TPU v7x, 32 devices: a whole 2x2x4 slice. The times are simulated.
32 devices in a mesh: dp: 16 (over z, y, x), section: 2 (over core).
Axes of the slice: x: 2, y: 2, z: 4, core: 2. Of those that a mesh axis runs over, the one named last changes fastest.
Arguments:
- path_table: bfloat16 [512, 2048], replicated, may hold values from -6 to 6
- tokens: int32 [16, 8, 48], P('dp'), may hold values from 0 to 511
- assign: int32 [16, 8], P('dp'), may hold values from 0 to 7, each once within a row
- out_grad: bfloat16 [16, 2, 4, 48, 2048], P('dp'), may hold values from -6 to 6
- query_weights: bfloat16 [2, 2048, 128], P('section', 'dp'), may hold values from -1 to 24
- gain: bfloat16 [2, 2048], P('section', 'dp'), may hold values from 0.5 to 1.5
- scale: bfloat16 [2, 2048], P('section', 'dp'), may hold values from 0.14 to 1.82
Outputs:
- query_grad: float32 [2, 2048, 128], P('section', 'dp')
- gain_grad: float32 [2, 2048], P('section', 'dp')
- scale_grad: float32 [2, 2048], P('section', 'dp')
All inputs are finite; a program needn't handle non-finite values.
Results may differ from a plain program's by a relative error of at most 0.0031.
Values may be sent and summed in bfloat16 or wider, within the bound.
A program may use at most 64 MiB of HBM per device.

v0:
```python
import math

import jax
import jax.numpy as jnp
from jax import lax
from jax.sharding import PartitionSpec as P

HIGH = lax.Precision.HIGHEST


def shifted(block, axis, distance):
    devices = range(lax.axis_size(axis))
    route = [(i - distance, i) for i in devices if i - distance in devices]
    return lax.ppermute(block, axis, route)


def from_partner(value, axis, apart):
    return lax.ppermute(value, axis, [(i, i ^ 1 << apart) for i in range(lax.axis_size(axis))])


def block_apply(stream_in, query_map, gain_vec, scale_vec):
    batch_count, seq_len, model_width = stream_in.shape
    head_size = query_map.shape[1]
    head_count = model_width // head_size
    stream = stream_in.astype(jnp.float32)
    mean_square = jnp.mean(stream * stream, axis=-1, keepdims=True)
    normed = stream * lax.rsqrt(mean_square + 1e-05) * gain_vec
    normed = lax.optimization_barrier(normed.astype(jnp.bfloat16)).astype(jnp.float32)
    heads_in = normed.reshape(batch_count, seq_len, head_count, head_size)
    query_heads = query_map.reshape(head_count, head_size, head_size)
    queries = jnp.einsum("nshi,hij->nshj", heads_in, query_heads, precision=HIGH) * (
        1.0 / math.sqrt(head_size)
    )
    queries = lax.optimization_barrier(queries.astype(jnp.bfloat16)).astype(jnp.float32)
    scores = jnp.einsum("nshj,nthj->nhst", queries, heads_in, precision=HIGH)
    causal = lax.broadcasted_iota(jnp.int32, (seq_len, seq_len), 0) >= lax.broadcasted_iota(
        jnp.int32, (seq_len, seq_len), 1
    )
    scores = jnp.where(causal, scores, -1e30)
    row_max = jnp.max(scores, axis=-1, keepdims=True)
    raised = jnp.exp(scores - row_max)
    attend = raised / jnp.sum(raised, axis=-1, keepdims=True)
    attend = lax.optimization_barrier(attend.astype(jnp.bfloat16)).astype(jnp.float32)
    mixed = jnp.einsum("nhst,nthj->nshj", attend, heads_in, precision=HIGH).reshape(
        batch_count, seq_len, model_width
    )
    return (stream + scale_vec * mixed).astype(jnp.bfloat16)


def pass_on(payload, offset):
    return shifted(payload, "section", offset)


def mirror(first_part, second_part, third_part):
    bit_count = lax.axis_size("section").bit_length() - 1
    for bit_index in range(bit_count):
        first_part, second_part, third_part = from_partner(
            (first_part, second_part, third_part), "section", bit_index
        )
    return (first_part, second_part, third_part)


def reduce_over_data(query_part, gain_part, scale_part):
    return (
        lax.psum_scatter(query_part, "dp", scatter_dimension=1, tiled=True),
        lax.psum_scatter(gain_part, "dp", scatter_dimension=1, tiled=True),
        lax.psum_scatter(scale_part, "dp", scatter_dimension=1, tiled=True),
    )


def apply_one(rows_in, params_in):
    return block_apply(rows_in[None], params_in[0], params_in[1], params_in[2])[0]


def on_device(path_table, tokens, assign, out_grad, query_weights, gain, scale):
    section_count = lax.axis_size("section")
    section_index = lax.axis_index("section")
    micro_count = out_grad.shape[2]
    slot_tokens = jnp.take(tokens[0], assign[0], axis=0)
    inputs = jnp.take(path_table, slot_tokens, axis=0)
    cotangents = out_grad[0]
    mirror_query, mirror_gain, mirror_scale = mirror(
        query_weights.astype(jnp.float32), gain.astype(jnp.float32), scale.astype(jnp.float32)
    )
    gathered = (
        lax.all_gather(query_weights, "dp", axis=1, tiled=True),
        lax.all_gather(gain, "dp", axis=1, tiled=True),
        lax.all_gather(scale, "dp", axis=1, tiled=True),
        lax.all_gather(mirror_query.astype(jnp.bfloat16), "dp", axis=1, tiled=True),
        lax.all_gather(mirror_gain.astype(jnp.bfloat16), "dp", axis=1, tiled=True),
        lax.all_gather(mirror_scale.astype(jnp.bfloat16), "dp", axis=1, tiled=True),
    )
    down_params = (
        gathered[0][0].astype(jnp.float32),
        gathered[1][0].astype(jnp.float32),
        gathered[2][0].astype(jnp.float32),
    )
    up_params = (
        gathered[3][0].astype(jnp.float32),
        gathered[4][0].astype(jnp.float32),
        gathered[5][0].astype(jnp.float32),
    )
    zero_rows = jnp.zeros(inputs.shape[1:], jnp.bfloat16)
    empty_store = jnp.zeros((micro_count,) + inputs.shape[1:], jnp.bfloat16)
    tick_count = micro_count + section_count - 1

    def run_if(live_flag, rows_in, params_in):
        return lax.cond(live_flag, lambda: apply_one(rows_in, params_in), lambda: zero_rows)

    def forward_tick(tick_index, state_tuple):
        recv_down, recv_up, store_down, store_up = state_tuple
        step_down = tick_index - section_index
        step_up = tick_index - (section_count - 1 - section_index)
        live_down = (step_down >= 0) & (step_down < micro_count)
        live_up = (step_up >= 0) & (step_up < micro_count)
        slot_down = jnp.clip(step_down, 0, micro_count - 1)
        slot_up = jnp.clip(step_up, 0, micro_count - 1)
        enter_down = lax.dynamic_index_in_dim(inputs, slot_down, 0, keepdims=False)
        enter_up = lax.dynamic_index_in_dim(inputs, slot_up + micro_count, 0, keepdims=False)
        input_down = jnp.where(section_index == 0, enter_down, recv_down)
        input_up = jnp.where(section_index == section_count - 1, enter_up, recv_up)
        output_down = run_if(live_down, input_down, down_params)
        output_up = run_if(live_up, input_up, up_params)
        store_down = jnp.where(
            live_down,
            lax.dynamic_update_index_in_dim(store_down, input_down, slot_down, 0),
            store_down,
        )
        store_up = jnp.where(
            live_up, lax.dynamic_update_index_in_dim(store_up, input_up, slot_up, 0), store_up
        )
        return (pass_on(output_down, 1), pass_on(output_up, -1), store_down, store_up)

    forward_state = lax.fori_loop(
        0, tick_count, forward_tick, (zero_rows, zero_rows, empty_store, empty_store)
    )
    saved_down, saved_up = (forward_state[2], forward_state[3])

    def pull_back(rows_in, cotangent, params_in):
        _, pullback = jax.vjp(apply_one, rows_in, params_in)
        return pullback(cotangent)

    def pull_if(live_flag, rows_in, cotangent, params_in):
        return lax.cond(
            live_flag,
            lambda: pull_back(rows_in, cotangent, params_in),
            lambda: (zero_rows, jax.tree.map(jnp.zeros_like, params_in)),
        )

    def backward_tick(tick_index, state_tuple):
        recv_down, recv_up, grads_down, grads_up = state_tuple
        step_down = tick_index - (section_count - 1 - section_index)
        step_up = tick_index - section_index
        live_down = (step_down >= 0) & (step_down < micro_count)
        live_up = (step_up >= 0) & (step_up < micro_count)
        slot_down = jnp.clip(step_down, 0, micro_count - 1)
        slot_up = jnp.clip(step_up, 0, micro_count - 1)
        given_down = lax.dynamic_index_in_dim(cotangents[0], slot_down, 0, keepdims=False)
        given_up = lax.dynamic_index_in_dim(cotangents[1], slot_up, 0, keepdims=False)
        cotangent_down = jnp.where(section_index == section_count - 1, given_down, recv_down)
        cotangent_up = jnp.where(section_index == 0, given_up, recv_up)
        back_down, delta_down = pull_if(
            live_down,
            lax.dynamic_index_in_dim(saved_down, slot_down, 0, keepdims=False),
            cotangent_down,
            down_params,
        )
        back_up, delta_up = pull_if(
            live_up,
            lax.dynamic_index_in_dim(saved_up, slot_up, 0, keepdims=False),
            cotangent_up,
            up_params,
        )
        grads_down = jax.tree.map(lambda before, added: before + added, grads_down, delta_down)
        grads_up = jax.tree.map(lambda before, added: before + added, grads_up, delta_up)
        return (pass_on(back_down, -1), pass_on(back_up, 1), grads_down, grads_up)

    empty_grads = jax.tree.map(jnp.zeros_like, down_params)
    backward_state = lax.fori_loop(
        0, tick_count, backward_tick, (zero_rows, zero_rows, empty_grads, empty_grads)
    )
    grads_down, grads_up = (backward_state[2], backward_state[3])
    stacked = reduce_over_data(
        jnp.stack([grads_down[0], grads_up[0]]),
        jnp.stack([grads_down[1], grads_up[1]]),
        jnp.stack([grads_down[2], grads_up[2]]),
    )
    moved = mirror(stacked[0][1], stacked[1][1], stacked[2][1])
    totals = (stacked[0][0] + moved[0], stacked[1][0] + moved[1], stacked[2][0] + moved[2])
    squares = (
        jnp.sum(totals[0] * totals[0])
        + jnp.sum(totals[1] * totals[1])
        + jnp.sum(totals[2] * totals[2])
    )
    overall = lax.psum(squares, ("dp", "section"))
    model_width = path_table.shape[1]
    head_size = query_weights.shape[2]
    limit = float(section_count * model_width * (head_size + 2))
    factor = jnp.minimum(1.0, math.sqrt(limit) / jnp.sqrt(overall))
    return ((totals[0] * factor)[None], (totals[1] * factor)[None], (totals[2] * factor)[None])


def solution(mesh):
    in_specs = (
        P(),
        P("dp", None, None),
        P("dp", None),
        P("dp", None, None, None, None),
        P("section", "dp", None),
        P("section", "dp"),
        P("section", "dp"),
    )
    out_specs = (P("section", "dp", None), P("section", "dp"), P("section", "dp"))
    return jax.shard_map(
        on_device, mesh=mesh, in_specs=in_specs, out_specs=out_specs, check_vma=False
    )
```

profile of v0, /device:TPU:0, one launch (start us, length us, event | category | flops | bytes accessed | tf_op | source)
XLA Modules:
  0.0 821.3 jit_solution(6334603760473554281)
XLA Ops:
  11.0 47.3 %all_gather.20 = bf16[1,2048,128]{2,1,0:T(8,128)(2,1)} all-gather(bf16[1,128,128]{2,1,0:T(8,128)(2,1)} %param.23), channel_id=1, replica_groups=mesh['dp'=16,'section'=2] {'dp'}, dimensions={1}, use_global_device_ids=true | all-gather | bytes 557056 | tf_op jit(solution)/shard_map/all_gather | solution.py:86
  65.1 35.5 %all_gather.19 = bf16[1,2048]{1,0:T(2,128)(2,1)S(1)} all-gather(bf16[1,128]{1,0:T(2,128)(2,1)S(1)} %copy-done.24), channel_id=1, replica_groups=mesh['dp'=16,'section'=2] {'dp'}, dimensions={1}, use_global_device_ids=true | all-gather | bytes 4352 | tf_op jit(solution)/shard_map/all_gather | solution.py:87
  100.6 37.5 %all_gather.18 = bf16[1,2048]{1,0:T(2,128)(2,1)S(1)} all-gather(bf16[1,128]{1,0:T(2,128)(2,1)S(1)} %copy-done.25), channel_id=1, replica_groups=mesh['dp'=16,'section'=2] {'dp'}, dimensions={1}, use_global_device_ids=true | all-gather | bytes 4352 | tf_op jit(solution)/shard_map/all_gather | solution.py:88
  138.7 35.5 %all_gather.22 = bf16[1,2048]{1,0:T(2,128)(2,1)S(1)} all-gather(bf16[1,128]{1,0:T(2,128)(2,1)S(1)} %collective-permute-done.5), channel_id=1, replica_groups=mesh['dp'=16,'section'=2] {'dp'}, dimensions={1}, use_global_device_ids=true | all-gather | bytes 4352 | tf_op jit(solution)/shard_map/all_gather | solution.py:90
  174.2 37.5 %all_gather.21 = bf16[1,2048]{1,0:T(2,128)(2,1)S(1)} all-gather(bf16[1,128]{1,0:T(2,128)(2,1)S(1)} %collective-permute-done.4), channel_id=1, replica_groups=mesh['dp'=16,'section'=2] {'dp'}, dimensions={1}, use_global_device_ids=true | all-gather | bytes 4352 | tf_op jit(solution)/shard_map/all_gather | solution.py:91
  212.3 38.2 %all_gather.23 = bf16[1,2048,128]{2,1,0:T(8,128)(2,1)S(1)} all-gather(bf16[1,128,128]{2,1,0:T(8,128)(2,1)S(1)} %collective-permute-done.6), channel_id=1, replica_groups=mesh['dp'=16,'section'=2] {'dp'}, dimensions={1}, use_global_device_ids=true | all-gather | bytes 557056 | tf_op jit(solution)/shard_map/all_gather | solution.py:89
  254.9 104.6 %while.50 = (s32[]{:T(128)}, bf16[48,2048]{1,0:T(8,128)(2,1)}, bf16[48,2048]{1,0:T(8,128)(2,1)}, bf16[4,48,2048]{2,1,0:T(8,128)(2,1)}, bf16[4,48,2048]{2,1,0:T(8...) while((s32[]{:T(128)}, bf16[48,2048]{1,0:T(8,128)(2,1)}, ...), condition=%wide.region_11.12_spmd, body=%wide.region_0.11_spmd.sunk | while | flops 342990656 | bytes 16068741 | solution.py:134
  259.1 6.1 conditional.10
  270.7 7.5 conditional.11
  279.5 6.1 conditional.10
  293.5 7.5 conditional.11
  302.3 6.1 conditional.10
  316.2 7.5 conditional.11
  325.0 6.1 conditional.10
  339.0 7.5 conditional.11
  348.5 9.1 %collective-permute-start = (bf16[48,2048]{1,0:T(8,128)(2,1)}, bf16[48,2048]{1,0:T(8,128)(2,1)S(1)}, u32[]{:S(2)}, u32[]{:S(2)}) collective-permute-start(bf16[48,2048]{1,0:T(8,128)(2,1)} %get-tuple-element.1541), channel_id=1, source_target_pairs={{0,1},{2,3},{4,5},{6,7},{8,9},{10,11},{12,13},{14,15},{16,17},{18,... | collective-permute-start | bytes 589832 | tf_op jit(solution)/shard_map/while/body/eval_jaxpr/ppermute | solution.py:14
  359.6 174.0 %while.51 = (s32[]{:T(128)}, bf16[48,2048]{1,0:T(8,128)(2,1)S(1)}, bf16[48,2048]{1,0:T(8,128)(2,1)S(1)}, f32[2048,128]{1,0:T(8,128)}, f32[2048]{0:T(1024)}, /*in...) while((s32[]{:T(128)}, bf16[48,2048]{1,0:T(8,128)(2,1)S(1)}, ...), condition=%wide.region_35.36_spmd.clone, body=%wide.region_12.35_spmd.clone.sunk | while | flops 1408627712 | bytes 66575548 | solution.py:179
  364.1 13.7 %conditional.13 = (bf16[48,2048]{1,0:T(8,128)(2,1)}, f32[2048,128]{1,0:T(8,128)}, f32[2048]{0:T(1024)S(1)}, f32[2048]{0:T(1024)}) conditional(s32[]{:T(128)} %convert_element_type.663, () %tuple.156, (pred[]{:T(512)}, bf16[2,4,48,2048]{3,2,1,0:T(8,128)(2,1)}, s32[]{:T(128)}, bf16[48,2048]{1,0:T(8,128)(2,1)S(1)}, f32[2048]{0:T(1024)}, ...), branch_computations={%region_24.24_spmd, %region_25.34_spmd} | conditional | flops 703781376 | bytes 31272188 | solution.py:144
  384.8 12.2 %conditional.12 = (bf16[48,2048]{1,0:T(8,128)(2,1)}, f32[2048,128]{1,0:T(8,128)}, f32[2048]{0:T(1024)S(1)}, f32[2048]{0:T(1024)}) conditional(s32[]{:T(128)} %convert_element_type.662, () %tuple.154, (pred[]{:T(512)}, bf16[2,4,48,2048]{3,2,1,0:T(8,128)(2,1)}, s32[]{:T(128)}, bf16[48,2048]{1,0:T(8,128)(2,1)S(1)}, f32[2048]{0:T(1024)}, ...), branch_computations={%region_13.13_spmd, %region_14.23_spmd} | conditional | flops 703781376 | bytes 27077856 | solution.py:144
  398.9 13.7 %conditional.13 = (bf16[48,2048]{1,0:T(8,128)(2,1)}, f32[2048,128]{1,0:T(8,128)}, f32[2048]{0:T(1024)S(1)}, f32[2048]{0:T(1024)}) conditional(s32[]{:T(128)} %convert_element_type.663, () %tuple.156, (pred[]{:T(512)}, bf16[2,4,48,2048]{3,2,1,0:T(8,128)(2,1)}, s32[]{:T(128)}, bf16[48,2048]{1,0:T(8,128)(2,1)S(1)}, f32[2048]{0:T(1024)}, ...), branch_computations={%region_24.24_spmd, %region_25.34_spmd} | conditional | flops 703781376 | bytes 31272188 | solution.py:144
  417.6 3.8 select_add_fusion.9
  422.0 12.2 %conditional.12 = (bf16[48,2048]{1,0:T(8,128)(2,1)}, f32[2048,128]{1,0:T(8,128)}, f32[2048]{0:T(1024)S(1)}, f32[2048]{0:T(1024)}) conditional(s32[]{:T(128)} %convert_element_type.662, () %tuple.154, (pred[]{:T(512)}, bf16[2,4,48,2048]{3,2,1,0:T(8,128)(2,1)}, s32[]{:T(128)}, bf16[48,2048]{1,0:T(8,128)(2,1)S(1)}, f32[2048]{0:T(1024)}, ...), branch_computations={%region_13.13_spmd, %region_14.23_spmd} | conditional | flops 703781376 | bytes 27077856 | solution.py:144
  436.0 13.7 %conditional.13 = (bf16[48,2048]{1,0:T(8,128)(2,1)}, f32[2048,128]{1,0:T(8,128)}, f32[2048]{0:T(1024)S(1)}, f32[2048]{0:T(1024)}) conditional(s32[]{:T(128)} %convert_element_type.663, () %tuple.156, (pred[]{:T(512)}, bf16[2,4,48,2048]{3,2,1,0:T(8,128)(2,1)}, s32[]{:T(128)}, bf16[48,2048]{1,0:T(8,128)(2,1)S(1)}, f32[2048]{0:T(1024)}, ...), branch_computations={%region_24.24_spmd, %region_25.34_spmd} | conditional | flops 703781376 | bytes 31272188 | solution.py:144
  454.7 3.8 select_add_fusion.9
  459.2 12.2 %conditional.12 = (bf16[48,2048]{1,0:T(8,128)(2,1)}, f32[2048,128]{1,0:T(8,128)}, f32[2048]{0:T(1024)S(1)}, f32[2048]{0:T(1024)}) conditional(s32[]{:T(128)} %convert_element_type.662, () %tuple.154, (pred[]{:T(512)}, bf16[2,4,48,2048]{3,2,1,0:T(8,128)(2,1)}, s32[]{:T(128)}, bf16[48,2048]{1,0:T(8,128)(2,1)S(1)}, f32[2048]{0:T(1024)}, ...), branch_computations={%region_13.13_spmd, %region_14.23_spmd} | conditional | flops 703781376 | bytes 27077856 | solution.py:144
  473.2 13.7 %conditional.13 = (bf16[48,2048]{1,0:T(8,128)(2,1)}, f32[2048,128]{1,0:T(8,128)}, f32[2048]{0:T(1024)S(1)}, f32[2048]{0:T(1024)}) conditional(s32[]{:T(128)} %convert_element_type.663, () %tuple.156, (pred[]{:T(512)}, bf16[2,4,48,2048]{3,2,1,0:T(8,128)(2,1)}, s32[]{:T(128)}, bf16[48,2048]{1,0:T(8,128)(2,1)S(1)}, f32[2048]{0:T(1024)}, ...), branch_computations={%region_24.24_spmd, %region_25.34_spmd} | conditional | flops 703781376 | bytes 31272188 | solution.py:144
  496.4 12.2 %conditional.12 = (bf16[48,2048]{1,0:T(8,128)(2,1)}, f32[2048,128]{1,0:T(8,128)}, f32[2048]{0:T(1024)S(1)}, f32[2048]{0:T(1024)}) conditional(s32[]{:T(128)} %convert_element_type.662, () %tuple.154, (pred[]{:T(512)}, bf16[2,4,48,2048]{3,2,1,0:T(8,128)(2,1)}, s32[]{:T(128)}, bf16[48,2048]{1,0:T(8,128)(2,1)S(1)}, f32[2048]{0:T(1024)}, ...), branch_computations={%region_13.13_spmd, %region_14.23_spmd} | conditional | flops 703781376 | bytes 27077856 | solution.py:144
  513.4 14.3 %collective-permute-start.3 = (bf16[48,2048]{1,0:T(8,128)(2,1)}, bf16[48,2048]{1,0:T(8,128)(2,1)S(1)}, u32[]{:S(2)}, u32[]{:S(2)}) collective-permute-start(bf16[48,2048]{1,0:T(8,128)(2,1)} %get-tuple-element.1374), channel_id=1, source_target_pairs={{0,1},{2,3},{4,5},{6,7},{8,9},{10,11},{12,13},{14,15},{16,17},{18,... | collective-permute-start | bytes 589832 | tf_op jit(solution)/shard_map/while/body/eval_jaxpr/ppermute | solution.py:14
  540.0 72.3 %reduce-scatter.12.cloned.1.call-done = f32[128,2]{1,0:T(8,128)} async-done(((f32[2048,2]{1,0:T(8,128)}), f32[128,2]{1,0:T(8,128)}) %reduce-scatter.12.cloned.1.call-update) | async-done | bytes 1040
  613.4 76.0 %reduce-scatter.10.cloned.1.call-done = f32[128,2]{1,0:T(8,128)} async-done(((f32[2048,2]{1,0:T(8,128)}), f32[128,2]{1,0:T(8,128)}) %reduce-scatter.10.cloned.1.call-update) | async-done | bytes 1040
  691.3 78.4 %reduce-scatter.8.cloned.1.call-done = f32[2,128,128]{2,1,0:T(8,128)} async-done(((f32[2,2048,128]{2,1,0:T(8,128)}), f32[2,128,128]{2,1,0:T(8,128)}) %reduce-scatter.8.cloned.1.call-update) | async-done | bytes 131088 | tf_op jit(solution)/shard_map/reduce_scatter | solution.py:65
  775.2 36.8 %psum.7 = f32[]{:T(128)} all-reduce(f32[]{:T(128)S(6)} %add.253), channel_id=1, replica_groups=mesh['dp'=16,'section'=2] {'dp','section'}, use_global_device_ids=true, to_apply=%region_42.43 | all-reduce | flops 1 | bytes 8 | tf_op jit(solution)/shard_map/psum | solution.py:195
  (645 shorter events, 281.7 us)
Async XLA Ops:
  7.2 51.3 %copy-start = (bf16[512,2048]{1,0:T(8,128)(2,1)S(1)}, bf16[512,2048]{1,0:T(8,128)(2,1)}, u32[]{:S(2)}) copy-start(bf16[512,2048]{1,0:T(8,128)(2,1)} %param.19) | copy-start | bytes 6291460
  7.2 605.1 %reduce-scatter.12.cloned.1.call-start = ((), (), s32[]{:S(2)}) async-start(), calls=%async_computation.5 | async-start | bytes 1114112
  7.2 131.4 %collective-permute-start.5 = (bf16[1,128]{1,0:T(2,128)(2,1)}, bf16[1,128]{1,0:T(2,128)(2,1)S(1)}, u32[]{:S(2)}, u32[]{:S(2)}) collective-permute-start(bf16[1,128]{1,0:T(2,128)(2,1)} %param.24), channel_id=1, source_target_pairs={{0,1},{1,0},{2,3},{3,2},{4,5},{5,4},{6,7},{7,6},{8,9},{9,8},{10,11... | collective-permute-start | bytes 776 | tf_op jit(solution)/shard_map/ppermute | solution.py:18
  7.8 166.4 %collective-permute-start.4 = (bf16[1,128]{1,0:T(2,128)(2,1)}, bf16[1,128]{1,0:T(2,128)(2,1)S(1)}, u32[]{:S(2)}, u32[]{:S(2)}) collective-permute-start(bf16[1,128]{1,0:T(2,128)(2,1)} %param.25), channel_id=1, source_target_pairs={{0,1},{1,0},{2,3},{3,2},{4,5},{5,4},{6,7},{7,6},{8,9},{9,8},{10,11... | collective-permute-start | bytes 776 | tf_op jit(solution)/shard_map/ppermute | solution.py:18
  7.9 204.4 %collective-permute-start.6 = (bf16[1,128,128]{2,1,0:T(8,128)(2,1)}, bf16[1,128,128]{2,1,0:T(8,128)(2,1)S(1)}, u32[]{:S(2)}, u32[]{:S(2)}) collective-permute-start(bf16[1,128,128]{2,1,0:T(8,128)(2,1)} %param.23), channel_id=1, source_target_pairs={{0,1},{1,0},{2,3},{3,2},{4,5},{5,4},{6,7},{7,6},{8,9},{9,8},{10,11... | collective-permute-start | bytes 98312 | tf_op jit(solution)/shard_map/ppermute | solution.py:18
  64.4 36.1 %copy-start.25 = (bf16[1,128]{1,0:T(2,128)(2,1)S(1)}, bf16[1,128]{1,0:T(2,128)(2,1)}, u32[]{:S(2)}) copy-start(bf16[1,128]{1,0:T(2,128)(2,1)} %param.25) | copy-start | bytes 772
  257.8 8.7 %collective-permute-start.1 = (bf16[48,2048]{1,0:T(8,128)(2,1)}, bf16[48,2048]{1,0:T(8,128)(2,1)}, u32[]{:S(2)}, u32[]{:S(2)}) collective-permute-start(bf16[48,2048]{1,0:T(8,128)(2,1)} %get-tuple-element.1542), channel_id=1, source_target_pairs={{1,0},{3,2},{5,4},{7,6},{9,8},{11,10},{13,12},{15,14},{17,16},{19,... | collective-permute-start | bytes 589832 | tf_op jit(solution)/shard_map/while/body/eval_jaxpr/ppermute | solution.py:14
  265.2 2.5 collective-permute-start
  278.2 11.1 %collective-permute-start.1 = (bf16[48,2048]{1,0:T(8,128)(2,1)}, bf16[48,2048]{1,0:T(8,128)(2,1)}, u32[]{:S(2)}, u32[]{:S(2)}) collective-permute-start(bf16[48,2048]{1,0:T(8,128)(2,1)} %get-tuple-element.1542), channel_id=1, source_target_pairs={{1,0},{3,2},{5,4},{7,6},{9,8},{11,10},{13,12},{15,14},{17,16},{19,... | collective-permute-start | bytes 589832 | tf_op jit(solution)/shard_map/while/body/eval_jaxpr/ppermute | solution.py:14
  285.6 4.9 collective-permute-start
  301.0 11.1 %collective-permute-start.1 = (bf16[48,2048]{1,0:T(8,128)(2,1)}, bf16[48,2048]{1,0:T(8,128)(2,1)}, u32[]{:S(2)}, u32[]{:S(2)}) collective-permute-start(bf16[48,2048]{1,0:T(8,128)(2,1)} %get-tuple-element.1542), channel_id=1, source_target_pairs={{1,0},{3,2},{5,4},{7,6},{9,8},{11,10},{13,12},{15,14},{17,16},{19,... | collective-permute-start | bytes 589832 | tf_op jit(solution)/shard_map/while/body/eval_jaxpr/ppermute | solution.py:14
  308.4 4.9 collective-permute-start
  323.7 11.1 %collective-permute-start.1 = (bf16[48,2048]{1,0:T(8,128)(2,1)}, bf16[48,2048]{1,0:T(8,128)(2,1)}, u32[]{:S(2)}, u32[]{:S(2)}) collective-permute-start(bf16[48,2048]{1,0:T(8,128)(2,1)} %get-tuple-element.1542), channel_id=1, source_target_pairs={{1,0},{3,2},{5,4},{7,6},{9,8},{11,10},{13,12},{15,14},{17,16},{19,... | collective-permute-start | bytes 589832 | tf_op jit(solution)/shard_map/while/body/eval_jaxpr/ppermute | solution.py:14
  331.1 4.9 collective-permute-start
  346.5 11.1 %collective-permute-start.1 = (bf16[48,2048]{1,0:T(8,128)(2,1)}, bf16[48,2048]{1,0:T(8,128)(2,1)}, u32[]{:S(2)}, u32[]{:S(2)}) collective-permute-start(bf16[48,2048]{1,0:T(8,128)(2,1)} %get-tuple-element.1542), channel_id=1, source_target_pairs={{1,0},{3,2},{5,4},{7,6},{9,8},{11,10},{13,12},{15,14},{17,16},{19,... | collective-permute-start | bytes 589832 | tf_op jit(solution)/shard_map/while/body/eval_jaxpr/ppermute | solution.py:14
  348.5 10.4 %collective-permute-start = (bf16[48,2048]{1,0:T(8,128)(2,1)}, bf16[48,2048]{1,0:T(8,128)(2,1)S(1)}, u32[]{:S(2)}, u32[]{:S(2)}) collective-permute-start(bf16[48,2048]{1,0:T(8,128)(2,1)} %get-tuple-element.1541), channel_id=1, source_target_pairs={{0,1},{2,3},{4,5},{6,7},{8,9},{10,11},{12,13},{14,15},{16,17},{18,... | collective-permute-start | bytes 589832 | tf_op jit(solution)/shard_map/while/body/eval_jaxpr/ppermute | solution.py:14
  362.8 21.4 %collective-permute-start.2 = (bf16[48,2048]{1,0:T(8,128)(2,1)}, bf16[48,2048]{1,0:T(8,128)(2,1)S(1)}, u32[]{:S(2)}, u32[]{:S(2)}) collective-permute-start(bf16[48,2048]{1,0:T(8,128)(2,1)} %get-tuple-element.1373), channel_id=1, source_target_pairs={{1,0},{3,2},{5,4},{7,6},{9,8},{11,10},{13,12},{15,14},{17,16},{19,... | collective-permute-start | bytes 589832 | tf_op jit(solution)/shard_map/while/body/eval_jaxpr/ppermute | solution.py:14
  378.3 5.9 collective-permute-start.3
  397.6 23.9 %collective-permute-start.2 = (bf16[48,2048]{1,0:T(8,128)(2,1)}, bf16[48,2048]{1,0:T(8,128)(2,1)S(1)}, u32[]{:S(2)}, u32[]{:S(2)}) collective-permute-start(bf16[48,2048]{1,0:T(8,128)(2,1)} %get-tuple-element.1373), channel_id=1, source_target_pairs={{1,0},{3,2},{5,4},{7,6},{9,8},{11,10},{13,12},{15,14},{17,16},{19,... | collective-permute-start | bytes 589832 | tf_op jit(solution)/shard_map/while/body/eval_jaxpr/ppermute | solution.py:14
  413.1 8.3 %collective-permute-start.3 = (bf16[48,2048]{1,0:T(8,128)(2,1)}, bf16[48,2048]{1,0:T(8,128)(2,1)S(1)}, u32[]{:S(2)}, u32[]{:S(2)}) collective-permute-start(bf16[48,2048]{1,0:T(8,128)(2,1)} %get-tuple-element.1374), channel_id=1, source_target_pairs={{0,1},{2,3},{4,5},{6,7},{8,9},{10,11},{12,13},{14,15},{16,17},{18,... | collective-permute-start | bytes 589832 | tf_op jit(solution)/shard_map/while/body/eval_jaxpr/ppermute | solution.py:14
  417.5 3.8 copy-start.20
  434.7 23.9 %collective-permute-start.2 = (bf16[48,2048]{1,0:T(8,128)(2,1)}, bf16[48,2048]{1,0:T(8,128)(2,1)S(1)}, u32[]{:S(2)}, u32[]{:S(2)}) collective-permute-start(bf16[48,2048]{1,0:T(8,128)(2,1)} %get-tuple-element.1373), channel_id=1, source_target_pairs={{1,0},{3,2},{5,4},{7,6},{9,8},{11,10},{13,12},{15,14},{17,16},{19,... | collective-permute-start | bytes 589832 | tf_op jit(solution)/shard_map/while/body/eval_jaxpr/ppermute | solution.py:14
  450.3 8.3 %collective-permute-start.3 = (bf16[48,2048]{1,0:T(8,128)(2,1)}, bf16[48,2048]{1,0:T(8,128)(2,1)S(1)}, u32[]{:S(2)}, u32[]{:S(2)}) collective-permute-start(bf16[48,2048]{1,0:T(8,128)(2,1)} %get-tuple-element.1374), channel_id=1, source_target_pairs={{0,1},{2,3},{4,5},{6,7},{8,9},{10,11},{12,13},{14,15},{16,17},{18,... | collective-permute-start | bytes 589832 | tf_op jit(solution)/shard_map/while/body/eval_jaxpr/ppermute | solution.py:14
  471.9 23.9 %collective-permute-start.2 = (bf16[48,2048]{1,0:T(8,128)(2,1)}, bf16[48,2048]{1,0:T(8,128)(2,1)S(1)}, u32[]{:S(2)}, u32[]{:S(2)}) collective-permute-start(bf16[48,2048]{1,0:T(8,128)(2,1)} %get-tuple-element.1373), channel_id=1, source_target_pairs={{1,0},{3,2},{5,4},{7,6},{9,8},{11,10},{13,12},{15,14},{17,16},{19,... | collective-permute-start | bytes 589832 | tf_op jit(solution)/shard_map/while/body/eval_jaxpr/ppermute | solution.py:14
  487.5 8.3 %collective-permute-start.3 = (bf16[48,2048]{1,0:T(8,128)(2,1)}, bf16[48,2048]{1,0:T(8,128)(2,1)S(1)}, u32[]{:S(2)}, u32[]{:S(2)}) collective-permute-start(bf16[48,2048]{1,0:T(8,128)(2,1)} %get-tuple-element.1374), channel_id=1, source_target_pairs={{0,1},{2,3},{4,5},{6,7},{8,9},{10,11},{12,13},{14,15},{16,17},{18,... | collective-permute-start | bytes 589832 | tf_op jit(solution)/shard_map/while/body/eval_jaxpr/ppermute | solution.py:14
  509.1 23.9 %collective-permute-start.2 = (bf16[48,2048]{1,0:T(8,128)(2,1)}, bf16[48,2048]{1,0:T(8,128)(2,1)S(1)}, u32[]{:S(2)}, u32[]{:S(2)}) collective-permute-start(bf16[48,2048]{1,0:T(8,128)(2,1)} %get-tuple-element.1373), channel_id=1, source_target_pairs={{1,0},{3,2},{5,4},{7,6},{9,8},{11,10},{13,12},{15,14},{17,16},{19,... | collective-permute-start | bytes 589832 | tf_op jit(solution)/shard_map/while/body/eval_jaxpr/ppermute | solution.py:14
  513.4 19.6 %collective-permute-start.3 = (bf16[48,2048]{1,0:T(8,128)(2,1)}, bf16[48,2048]{1,0:T(8,128)(2,1)S(1)}, u32[]{:S(2)}, u32[]{:S(2)}) collective-permute-start(bf16[48,2048]{1,0:T(8,128)(2,1)} %get-tuple-element.1374), channel_id=1, source_target_pairs={{0,1},{2,3},{4,5},{6,7},{8,9},{10,11},{12,13},{14,15},{16,17},{18,... | collective-permute-start | bytes 589832 | tf_op jit(solution)/shard_map/while/body/eval_jaxpr/ppermute | solution.py:14
  535.7 153.7 %reduce-scatter.10.cloned.1.call-start = ((), (), s32[]{:S(2)}) async-start(), calls=%async_computation.4 | async-start | bytes 1114112
  537.2 232.5 %reduce-scatter.8.cloned.1.call-start = ((), (), s32[]{:S(2)}) async-start(), calls=%async_computation.3 | async-start | bytes 2228224 | tf_op jit(solution)/shard_map/reduce_scatter | solution.py:65
  613.4 77.3 %collective-permute-start.9 = (f32[128]{0:T(128)S(1)}, f32[128]{0:T(128)S(1)}, u32[]{:S(2)}, u32[]{:S(2)}) collective-permute-start(f32[128]{0:T(128)S(1)} %bitcast.448), channel_id=1, source_target_pairs={{0,1},{1,0},{2,3},{3,2},{4,5},{5,4},{6,7},{7,6},{8,9},{9,8},{10,11... | collective-permute-start | bytes 1544 | tf_op jit(solution)/shard_map/ppermute | solution.py:18
  690.6 79.9 %collective-permute-start.8 = (f32[128]{0:T(128)S(1)}, f32[128]{0:T(128)S(1)}, u32[]{:S(2)}, u32[]{:S(2)}) collective-permute-start(f32[128]{0:T(128)S(1)} %bitcast.449), channel_id=1, source_target_pairs={{0,1},{1,0},{2,3},{3,2},{4,5},{5,4},{6,7},{7,6},{8,9},{9,8},{10,11... | collective-permute-start | bytes 1544 | tf_op jit(solution)/shard_map/ppermute | solution.py:18
  770.6 1.3 collective-permute-start.7
  (89 other events, 160.3 us)
Sparse Core Ops, SparseCore 0:
  535.9 76.4 reduce-scatter.11
  614.6 74.8 reduce-scatter.9
  691.7 77.9 reduce-scatter.7
where the time goes:
time: 825 us; the launch traced here: 821 us
  blocking collectives  268 us (32%)
  waiting for transfers between devices  234 us (28%)
  other arithmetic  112 us (14%)
  matrix products  85.9 us (10%)
  starting transfers between devices  60.2 us (7%)
  local copies, waits for them, and re-layouts  41.4 us (5%)
  between operations  16.5 us (2%)
    unnamed x5, waiting for transfers between devices  148 us
    reduce_scatter x1, waiting for transfers between devices, reduce_over_data(): lax.psum_scatter(query_part, 'dp', scatter_dimension=1, tiled=True)  78.4 us
    ppermute x20, starting transfers between devices, shifted(): return lax.ppermute(block, axis, route)  58.9 us
    all_gather x1, blocking collectives, on_device(): lax.all_gather(query_weights, 'dp', axis=1, tiled=True)  47.3 us
    dot_general x32, matrix products, block_apply(): jnp.einsum('nshi,hij->nshj', heads_in, query_heads, precision=HIGH)  46.9 us
    all_gather x1, blocking collectives, on_device(): lax.all_gather(mirror_query.astype(jnp.bfloat16), 'dp', axis=1, tiled=True)  38.2 us
    all_gather x1, blocking collectives, on_device(): lax.all_gather(mirror_scale.astype(jnp.bfloat16), 'dp', axis=1, tiled=True)  37.5 us
    all_gather x1, blocking collectives, on_device(): lax.all_gather(scale, 'dp', axis=1, tiled=True)  37.5 us
  transfers between devices with their start and end apart: 29, of which 9 were waited for; matrix products, arithmetic and copies ran while one was open for 15% of the time, Pallas kernels for 0%

commit v1 on v0

v1 whole, which is shorter than its diff:
```python
import functools
import math

import jax
import jax.numpy as jnp
from jax import lax
from jax.experimental import pallas as pl
from jax.experimental.pallas import tpu as pltpu
from jax.sharding import PartitionSpec as P

MESH = pl.DeviceIdType.MESH
F32 = jnp.float32
BF16 = jnp.bfloat16
TAIL = 16
GROUP = 2


def matmul(lhs, rhs, lhs_dim, rhs_dim):
    return lax.dot_general(
        lhs, rhs, (((lhs_dim,), (rhs_dim,)), ((), ())), preferred_element_type=F32
    )


def step_kernel(
    n_dp,
    n_sec,
    table,
    tokens,
    assign,
    out_grad,
    weights,
    gain,
    scale,
    query_out,
    gain_out,
    scale_out,
    packed,
    params,
    picked,
    tbl,
    cot,
    xs,
    normed,
    queries,
    mixed,
    probs,
    dnormed,
    acc,
    rstd,
    parts,
    tx,
    rx,
    norms,
    load_sem,
    w_send,
    w_recv,
    x_send,
    x_recv,
    g_send,
    g_recv,
    n_send,
    n_recv,
):
    slots, seq = tokens.shape
    heads, count, hd = cot.shape
    vocab, width = table.shape
    rows = weights.shape[0]
    layers = n_sec
    pieces = n_dp // n_sec
    per_head = hd // rows
    n_dev = n_dp * n_sec
    group_rows = GROUP * seq
    groups = slots // GROUP
    inv = 1.0 / math.sqrt(hd)
    me_d = lax.axis_index("dp")
    me_s = lax.axis_index("section")
    me = me_d * n_sec + me_s

    def columns(h):
        return pl.ds(pl.multiple_of((me_s * heads + h) * hd, hd), hd)

    def remote(src, dst, ssem, rsem, d, s):
        return pltpu.make_async_remote_copy(
            src_ref=src,
            dst_ref=dst,
            send_sem=ssem,
            recv_sem=rsem,
            device_id=(d, s),
            device_id_type=MESH,
        )

    for h in range(heads):
        pltpu.make_async_copy(table.at[:, columns(h)], tbl.at[h], load_sem.at[0]).start()
    for h in range(heads):
        pltpu.make_async_copy(out_grad.at[:, columns(h)], cot.at[h], load_sem.at[1]).start()

    barrier = pltpu.get_barrier_semaphore()

    def greet(k, carry):
        t = lax.rem(me + k, n_dev)
        pl.semaphore_signal(
            barrier,
            inc=1,
            device_id=(lax.div(t, n_sec), lax.rem(t, n_sec)),
            device_id_type=MESH,
        )
        return carry

    lax.fori_loop(1, n_dev, greet, 0)

    packed[0:rows, :] = weights[...]
    tail_row = lax.broadcasted_iota(jnp.int32, (TAIL, hd), 0)
    packed[rows : rows + TAIL, :] = jnp.where(
        tail_row == 0,
        gain[...].astype(F32),
        jnp.where(tail_row == 1, scale[...].astype(F32), 0.0),
    ).astype(BF16)

    eye = lax.broadcasted_iota(jnp.int32, (seq, seq), 0) == lax.broadcasted_iota(
        jnp.int32, (seq, seq), 1
    )
    vocab_lane = lax.broadcasted_iota(jnp.int32, (seq, vocab), 1).astype(F32)
    for j in range(slots):
        row = tokens[pl.ds(assign[j], 1), :].astype(F32)
        col = jnp.sum(jnp.where(eye, row, 0.0), axis=1, keepdims=True)
        picked[j * seq : (j + 1) * seq, :] = jnp.where(vocab_lane == col, 1.0, 0.0).astype(BF16)

    pl.semaphore_wait(barrier, n_dev - 1)

    owner = lax.div(me_d, pieces)
    place = lax.rem(me_d, pieces)
    keep = owner == me_s

    @pl.when(keep)
    def _():
        pltpu.make_async_copy(packed, params.at[me_s, place], w_recv.at[me_s]).start()

    @pl.when(jnp.logical_not(keep))
    def _():
        remote(packed, params.at[me_s, place], w_send, w_recv.at[me_s], me_d, owner).start()

    def give(k, carry):
        r = lax.rem(me_d + k, n_dp)
        remote(packed, params.at[me_s, place], w_send, w_recv.at[me_s], r, owner).start()
        return carry

    lax.fori_loop(1, n_dp, give, 0)

    lane = lax.broadcasted_iota(jnp.int32, (seq, hd), 1)

    def exchange(phase):
        sums = jnp.sum(acc[...], axis=1, keepdims=True)
        compact = jnp.zeros((seq, hd), F32)
        for j in range(slots):
            compact = jnp.where(lane == j, sums[j * seq : (j + 1) * seq], compact)
        parts[phase, pl.ds(me_s, 1)] = compact[None]
        for k in range(1, n_sec):
            s = lax.rem(me_s + k, n_sec)
            remote(
                parts.at[phase, me_s], parts.at[phase, me_s], x_send, x_recv.at[phase], me_d, s
            ).start()

    def exchanged(phase):
        if n_sec > 1:
            whole = parts.at[phase, pl.ds(0, n_sec - 1)]
            pltpu.make_async_copy(whole, whole, x_recv.at[phase]).wait()
        return jnp.sum(parts[phase], axis=0)

    def spread(compact, j):
        return jnp.broadcast_to(compact[:, j : j + 1], (seq, hd))

    def layer_param(b, h):
        block = params[b, pl.ds(h * per_head, per_head)]
        if per_head == 1:
            tail = block[0, rows:, :].astype(F32)
            weight = block[0, :rows, :]
        else:
            tail = block[0, rows:, :].astype(F32)
            for i in range(1, per_head):
                tail = tail + block[i, rows:, :].astype(F32)
            weight = jnp.concatenate([block[i, :rows, :] for i in range(per_head)], axis=0)
        return weight, tail[0:1], tail[1:2]

    pltpu.make_async_copy(tbl, tbl, load_sem.at[0]).wait()
    acc[...] = jnp.zeros_like(acc)

    def embed(h, carry):
        rows_in = matmul(picked[...], tbl[h], 1, 0)
        xs[0, h] = rows_in.astype(BF16)
        acc[...] += rows_in * rows_in
        return carry

    lax.fori_loop(0, heads, embed, 0)

    at_row = lax.broadcasted_iota(jnp.int32, (group_rows, group_rows), 0)
    at_col = lax.broadcasted_iota(jnp.int32, (group_rows, group_rows), 1)
    allowed = at_row >= at_col
    for i in range(1, GROUP):
        allowed = allowed & ((at_row >= i * seq) == (at_col >= i * seq))

    for b in range(layers):
        exchange(b)
        if b == 0:
            for i in range(layers):
                pltpu.make_async_copy(params.at[i], params.at[i], w_recv.at[i]).wait()
        root = lax.rsqrt(exchanged(b) * (1.0 / width) + 1e-05)
        for j in range(slots):
            rstd[b, j * seq : (j + 1) * seq, :] = spread(root, j)
        acc[...] = jnp.zeros_like(acc)

        def forward(h, carry):
            weight, gain_row, scale_row = layer_param(b, h)
            x_in = xs[b, h].astype(F32)
            norm = (x_in * rstd[b] * gain_row).astype(BF16)
            normed[b, h] = norm
            query = (matmul(norm, weight, 1, 0) * inv).astype(BF16)
            queries[b, h] = query
            for i in range(groups):
                lo, hi = i * group_rows, (i + 1) * group_rows
                scores = matmul(query[lo:hi], norm[lo:hi], 1, 1)
                scores = jnp.where(allowed, scores, -1e30)
                raised = jnp.exp(scores - jnp.max(scores, axis=1, keepdims=True))
                attend = raised * (1.0 / jnp.sum(raised, axis=1, keepdims=True))
                probs[b, h, i] = attend
                mix = matmul(attend.astype(BF16), norm[lo:hi], 1, 0)
                mixed[b, h, lo:hi] = mix
                if b + 1 < layers:
                    out = (x_in[lo:hi] + scale_row * mix).astype(BF16)
                    xs[b + 1, h, lo:hi] = out
                    out = out.astype(F32)
                    acc[lo:hi] += out * out
            return carry

        lax.fori_loop(0, heads, forward, 0)

    pltpu.make_async_copy(cot, cot, load_sem.at[1]).wait()

    for b in reversed(range(layers)):
        if b > 0:
            acc[...] = jnp.zeros_like(acc)

        def backward(h, carry):
            weight, gain_row, scale_row = layer_param(b, h)
            given = cot[h].astype(F32)
            scale_part = jnp.sum(given * mixed[b, h], axis=0, keepdims=True)
            norm = normed[b, h]
            query = queries[b, h]
            dmix = (given * scale_row).astype(BF16)
            dquery_parts, dnorm_parts = [], []
            for i in range(groups):
                lo, hi = i * group_rows, (i + 1) * group_rows
                attend = probs[b, h, i]
                dattend = matmul(dmix[lo:hi], norm[lo:hi], 1, 1).astype(BF16).astype(F32)
                inner = jnp.sum(dattend * attend, axis=1, keepdims=True)
                dscore = (attend * (dattend - inner)).astype(BF16)
                dquery_parts.append(matmul(dscore, norm[lo:hi], 1, 0).astype(BF16))
                left = jnp.concatenate([dscore, attend.astype(BF16)], axis=0)
                right = jnp.concatenate([query[lo:hi], dmix[lo:hi]], axis=0)
                dnorm_parts.append(matmul(left, right, 0, 0))
            dquery = jnp.concatenate(dquery_parts, axis=0)
            dnorm = jnp.concatenate(dnorm_parts, axis=0) + matmul(dquery, weight, 1, 1) * inv
            dweight = matmul(norm, dquery, 0, 0) * inv
            dnorm = dnorm.astype(BF16)
            if b > 0:
                dnormed[h] = dnorm
            dnorm = dnorm.astype(F32)
            x_in = xs[b, h].astype(F32)
            gain_part = jnp.sum(dnorm * (x_in * rstd[b]), axis=0, keepdims=True)
            if b > 0:
                acc[...] += dnorm * gain_row * x_in
            gain_hi = gain_part.astype(BF16).astype(F32)
            scale_hi = scale_part.astype(BF16).astype(F32)
            tail = jnp.where(
                tail_row == 0,
                gain_hi,
                jnp.where(
                    tail_row == 1,
                    gain_part - gain_hi,
                    jnp.where(
                        tail_row == 2,
                        scale_hi,
                        jnp.where(tail_row == 3, scale_part - scale_hi, 0.0),
                    ),
                ),
            ).astype(BF16)
            dweight = dweight.astype(BF16)
            for i in range(per_head):
                p = h * per_head + i
                tx[b, p, 0:rows] = dweight[i * rows : (i + 1) * rows]
                tx[b, p, rows : rows + TAIL] = tail
                r = me_s * pieces + p
                mine = (r == me_d) & (me_s == b)

                @pl.when(mine)
                def _():
                    pltpu.make_async_copy(tx.at[b, p], rx.at[me_d], g_recv).start()

                @pl.when(jnp.logical_not(mine))
                def _():
                    remote(tx.at[b, p], rx.at[me_d], g_send, g_recv, r, b).start()

            return carry

        lax.fori_loop(0, heads, backward, 0)
        if b > 0:
            phase = layers + b - 1
            exchange(phase)
            inner = exchanged(phase) * (1.0 / width)
            acc_rows = [spread(inner, j) for j in range(slots)]
            root = rstd[b]
            acc[...] = jnp.concatenate(acc_rows, axis=0) * root * root * root

            def stream_back(h, carry):
                _, gain_row, _ = layer_param(b, h)
                dy = dnormed[h].astype(F32) * gain_row
                back = rstd[b] * dy - xs[b, h].astype(F32) * acc[...]
                cot[h] = (cot[h].astype(F32) + back).astype(BF16)
                return carry

            lax.fori_loop(0, heads, stream_back, 0)

    pltpu.make_async_copy(rx, rx, g_recv).wait()
    total = jnp.sum(rx[...].astype(F32), axis=0)
    total_query = total[0:rows]
    total_gain = total[rows : rows + 1] + total[rows + 1 : rows + 2]
    total_scale = total[rows + 2 : rows + 3] + total[rows + 3 : rows + 4]
    if per_head > 1:
        at = lax.broadcasted_iota(jnp.int32, (1, hd), 1)
        first = lax.rem(me_d, per_head) * rows
        inside = (at >= first) & (at < first + rows)
        total_gain = jnp.where(inside, total_gain, 0.0)
        total_scale = jnp.where(inside, total_scale, 0.0)
    squares = (
        jnp.sum(total_query * total_query, axis=0, keepdims=True)
        + total_gain * total_gain
        + total_scale * total_scale
    )
    norms[pl.ds(me, 1)] = squares[None]

    def tell(k, carry):
        t = lax.rem(me + k, n_dev)
        remote(
            norms.at[me], norms.at[me], n_send, n_recv, lax.div(t, n_sec), lax.rem(t, n_sec)
        ).start()
        return carry

    lax.fori_loop(1, n_dev, tell, 0)
    others = norms.at[pl.ds(0, n_dev - 1)]
    pltpu.make_async_copy(others, others, n_recv).wait()
    overall = jnp.sum(jnp.sum(norms[...], axis=0), axis=1, keepdims=True)
    limit = float(layers * width * (hd + 2))
    factor = jnp.minimum(1.0, math.sqrt(limit) / jnp.sqrt(overall))
    query_out[...] = total_query * factor
    gain_out[...] = total_gain * factor
    scale_out[...] = total_scale * factor

    pltpu.make_async_copy(others, others, n_send).wait()
    if n_sec > 1:
        for phase in range(2 * layers - 1):
            whole = parts.at[phase, pl.ds(0, n_sec - 1)]
            pltpu.make_async_copy(whole, whole, x_send).wait()

    def sent_weight(k, carry):
        pltpu.make_async_copy(packed, packed, w_send).wait()
        return carry

    lax.fori_loop(0, jnp.where(keep, n_dp - 1, n_dp), sent_weight, 0)

    def sent_grad(k, carry):
        pltpu.make_async_copy(packed, packed, g_send).wait()
        return carry

    lax.fori_loop(0, jnp.where(keep, layers * pieces - 1, layers * pieces), sent_grad, 0)


def on_device(path_table, tokens, assign, out_grad, query_weights, gain, scale):
    n_dp = lax.axis_size("dp")
    n_sec = lax.axis_size("section")
    vocab, width = path_table.shape
    slots, seq = tokens.shape[1:]
    rows, hd = query_weights.shape[1:]
    count = slots * seq
    layers = n_sec
    heads = width // n_sec // hd
    pieces = n_dp // n_sec
    n_dev = n_dp * n_sec
    groups = slots // GROUP
    first = lax.rem(lax.axis_index("dp") * rows, hd)
    if rows < hd:
        gain = lax.dynamic_update_slice(jnp.zeros((1, hd), BF16), gain, (0, first))
        scale = lax.dynamic_update_slice(jnp.zeros((1, hd), BF16), scale, (0, first))
    vmem = pl.BlockSpec(memory_space=pltpu.VMEM)
    hbm = pl.BlockSpec(memory_space=pl.ANY)
    smem = pl.BlockSpec(memory_space=pltpu.SMEM)
    query_grad, gain_grad, scale_grad = pl.pallas_call(
        functools.partial(step_kernel, n_dp, n_sec),
        out_shape=(
            jax.ShapeDtypeStruct((rows, hd), F32),
            jax.ShapeDtypeStruct((1, hd), F32),
            jax.ShapeDtypeStruct((1, hd), F32),
        ),
        in_specs=[hbm, vmem, smem, hbm, vmem, vmem, vmem],
        out_specs=(vmem, vmem, vmem),
        scratch_shapes=[
            pltpu.VMEM((rows + TAIL, hd), BF16),
            pltpu.VMEM((layers, pieces, rows + TAIL, hd), BF16),
            pltpu.VMEM((count, vocab), BF16),
            pltpu.VMEM((heads, vocab, hd), BF16),
            pltpu.VMEM((heads, count, hd), BF16),
            pltpu.VMEM((layers, heads, count, hd), BF16),
            pltpu.VMEM((layers, heads, count, hd), BF16),
            pltpu.VMEM((layers, heads, count, hd), BF16),
            pltpu.VMEM((layers, heads, count, hd), F32),
            pltpu.VMEM((layers, heads, groups, GROUP * seq, GROUP * seq), F32),
            pltpu.VMEM((heads, count, hd), BF16),
            pltpu.VMEM((count, hd), F32),
            pltpu.VMEM((layers, count, hd), F32),
            pltpu.VMEM((2 * layers - 1, n_sec, seq, hd), F32),
            pltpu.VMEM((layers, pieces, rows + TAIL, hd), BF16),
            pltpu.VMEM((n_dp, rows + TAIL, hd), BF16),
            pltpu.VMEM((n_dev, 1, hd), F32),
            pltpu.SemaphoreType.DMA((2,)),
            pltpu.SemaphoreType.DMA,
            pltpu.SemaphoreType.DMA((layers,)),
            pltpu.SemaphoreType.DMA,
            pltpu.SemaphoreType.DMA((2 * layers - 1,)),
            pltpu.SemaphoreType.DMA,
            pltpu.SemaphoreType.DMA,
            pltpu.SemaphoreType.DMA,
            pltpu.SemaphoreType.DMA,
        ],
        compiler_params=pltpu.CompilerParams(
            collective_id=0, has_side_effects=True, vmem_limit_bytes=56 * 1024 * 1024
        ),
    )(
        path_table,
        tokens[0],
        assign[0],
        out_grad.reshape(count, width),
        query_weights[0],
        gain,
        scale,
    )
    if rows < hd:
        gain_grad = lax.dynamic_slice(gain_grad, (0, first), (1, rows))
        scale_grad = lax.dynamic_slice(scale_grad, (0, first), (1, rows))
    return query_grad[None], gain_grad, scale_grad


def solution(mesh):
    in_specs = (
        P(),
        P("dp", None, None),
        P("dp", None),
        P("dp", None, None, None, None),
        P("section", "dp", None),
        P("section", "dp"),
        P("section", "dp"),
    )
    out_specs = (P("section", "dp", None), P("section", "dp"), P("section", "dp"))
    return jax.shard_map(
        on_device, mesh=mesh, in_specs=in_specs, out_specs=out_specs, check_vma=False
    )
```

time: 825 us -> 74.2 us (0.09)
  blocking collectives: 268 us -> 0 us
  waiting for transfers between devices: 234 us -> 0 us
  other arithmetic: 112 us -> 0 us
  matrix products: 85.9 us -> 0 us
  Pallas kernels: 0 us -> 69.6 us
  starting transfers between devices: 60.2 us -> 0 us
  local copies, waits for them, and re-layouts: 41.4 us -> 3.7 us
  between operations: 16.5 us -> 0.64 us
    all_gather x6 -> x0, blocking collectives: 232 us -> none  [the longest x1 47.3 us: on_device(): lax.all_gather(query_weights, 'dp', axis=1, tiled=True)]
    unnamed x5 -> x0, waiting for transfers between devices: 148 us -> none
    dot_general x96 -> x0, matrix products: 85.9 us -> none  [the longest x32 46.9 us: block_apply(): jnp.einsum('nshi,hij->nshj', heads_in, query_heads, precision=HIGH)]
    reduce_scatter x1 -> x0, waiting for transfers between devices: 78.4 us -> none  [reduce_over_data(): lax.psum_scatter(query_part, 'dp', scatter_dimension=1, tiled=True)]
    pallas_call x0 -> x1, Pallas kernels: none -> 69.6 us  [on_device(): pl.pallas_call(functools.partial(step_kernel, n_dp, n_sec), out_shape=(ja...]
    ppermute x26 -> x0, starting transfers between devices: 60.1 us -> none  [the longest x20 58.9 us: shifted(): return lax.ppermute(block, axis, route)]
    psum x1 -> x0, blocking collectives: 36.8 us -> none  [on_device(): overall = lax.psum(squares, ('dp', 'section'))]
    reduce_sum x75 -> x0, other arithmetic: 31.4 us -> none  [the longest x16 9.73 us: block_apply(): mean_square = jnp.mean(stream * stream, axis=-1, keepdims=True)]
  transfers between devices with their start and end apart: 29 -> 0, of which waited for: 9 -> 0; matrix products, arithmetic and copies ran while one was open for 15% -> 0% of each run, Pallas kernels for 0% -> 0%
where the time goes in v1:
time: 74.2 us; the launch traced here: 73.9 us
  Pallas kernels  69.6 us (94%)
  local copies, waits for them, and re-layouts  3.7 us (5%)
    pallas_call x1, Pallas kernels, on_device(): pl.pallas_call(functools.partial(step_kernel, n_dp, n_sec), out_shape=(ja...  69.6 us
    unnamed x3, local copies, waits for them, and re-layouts  3.7 us

profile of v1, /device:TPU:0, one launch (start us, length us, event | category | flops | bytes accessed | tf_op | source)
XLA Modules:
  0.0 73.9 jit_solution(4540072089121772929)
XLA Ops:
  0.6 69.6 %shard_map.94 = (f32[128,128]{1,0:T(8,128)}, f32[1,128]{1,0:T(1,128)}, f32[1,128]{1,0:T(1,128)}) custom-call(bf16[512,2048]{1,0:T(8,128)(2,1)} %table.1, s32[8,48]{1,0:T(8,128)} %bitcast.8, s32[8]{0:T(128)} %bitcast.9, bf16[384,2048]{1,0:T(8,128)(2,1)} %bitcast.5, bf16[128,128]{1,0:T(8,128)(2,1)} %bitcast.7, bf16[1,128]{1,0:T(2,128)(2,1)} %gain.1, ...), custom_call_target="tpu_custom_call" | custom-call | tf_op jit(solution)/shard_map/pallas_call | solution.py:395
  70.2 1.5 %copy.13 = f32[1,128,128]{2,1,0:T(8,128)} copy(f32[1,128,128]{2,1,0:T(8,128)} %bitcast.6) | data formatting | bytes 131072
  71.7 1.1 %copy.14 = f32[1,128]{1,0:T(1,128)} copy(f32[1,128]{1,0:T(1,128)} %get-tuple-element.13) | data formatting | bytes 1024
  72.8 1.1 %copy.15 = f32[1,128]{1,0:T(1,128)} copy(f32[1,128]{1,0:T(1,128)} %get-tuple-element.14) | data formatting | bytes 1024

commit v2 on v1

v2 whole, which is shorter than its diff:
```python
import functools
import math

import jax
import jax.numpy as jnp
from jax import lax
from jax.experimental import pallas as pl
from jax.experimental.pallas import tpu as pltpu
from jax.sharding import PartitionSpec as P

MESH = pl.DeviceIdType.MESH
F32 = jnp.float32
BF16 = jnp.bfloat16
TAIL = 16
GROUP = 2
PLANE = 4


def matmul(lhs, rhs, lhs_dim, rhs_dim):
    return lax.dot_general(
        lhs, rhs, (((lhs_dim,), (rhs_dim,)), ((), ())), preferred_element_type=F32
    )


def layout(n_dp, n_sec, width, hd):
    plane = math.gcd(n_dp, min(PLANE, width // hd // n_sec))
    return plane, n_dp // plane, width // hd // n_sec // plane


def step_kernel(
    n_dp,
    n_sec,
    table,
    tokens,
    assign,
    out_grad,
    weights,
    gain,
    scale,
    query_out,
    gain_out,
    scale_out,
    packed,
    params,
    toks,
    picked,
    tbl,
    emb,
    cot,
    xs,
    normed,
    queries,
    mixed,
    probs,
    dnormed,
    acc,
    rstd,
    parts,
    grads,
    tails,
    tx,
    rx,
    norms,
    load_sem,
    t_send,
    t_recv,
    w_send,
    w_recv,
    c_send,
    c_recv,
    x_send,
    x_recv,
    g_send,
    g_recv,
    n_send,
    n_recv,
):
    slots, seq = tokens.shape
    vocab, width = table.shape
    rows, hd = weights.shape
    plane, planes, heads = layout(n_dp, n_sec, width, hd)
    layers = n_sec
    per_head = hd // rows
    n_dev = n_dp * n_sec
    members = plane * n_sec
    group_rows = GROUP * seq
    groups = slots // GROUP
    inv = 1.0 / math.sqrt(hd)
    me_d = lax.axis_index("dp")
    me_s = lax.axis_index("section")
    me = me_d * n_sec + me_s
    me_z = lax.div(me_d, plane)
    me_p = lax.rem(me_d, plane)
    member = me_p * n_sec + me_s

    def head_of(p, c, hh):
        return (c * heads + hh) * plane + p

    def columns(h):
        return pl.ds(pl.multiple_of(h * hd, hd), hd)

    def remote(src, dst, ssem, rsem, d, s):
        return pltpu.make_async_remote_copy(
            src_ref=src,
            dst_ref=dst,
            send_sem=ssem,
            recv_sem=rsem,
            device_id=(d, s),
            device_id_type=MESH,
        )

    pltpu.make_async_copy(table, tbl, load_sem).start()
    for hh in range(heads):
        pltpu.make_async_copy(
            out_grad.at[:, columns(head_of(me_p, me_s, hh))], cot.at[me_p, hh], c_recv.at[me_p]
        ).start()

    barrier = pltpu.get_barrier_semaphore()

    def greet(k, carry):
        t = lax.rem(me + k, n_dev)
        pl.semaphore_signal(
            barrier,
            inc=1,
            device_id=(lax.div(t, n_sec), lax.rem(t, n_sec)),
            device_id_type=MESH,
        )
        return carry

    lax.fori_loop(1, n_dev, greet, 0)

    packed[0:rows, :] = weights[...]
    tail_row = lax.broadcasted_iota(jnp.int32, (TAIL, hd), 0)
    packed[rows : rows + TAIL, :] = jnp.where(
        tail_row == 0,
        gain[...].astype(F32),
        jnp.where(tail_row == 1, scale[...].astype(F32), 0.0),
    ).astype(BF16)
    for j in range(slots):
        toks[me_p, j : j + 1, 0:seq] = tokens[pl.ds(assign[j], 1), :].astype(F32)

    pltpu.make_async_copy(tbl, tbl, load_sem).wait()
    chunk = math.gcd(vocab, 64)
    lane_chunk = lax.broadcasted_iota(jnp.int32, (chunk, hd), 1)

    def table_norm(i, carry):
        at = pl.ds(pl.multiple_of(i * chunk, chunk), chunk)
        squares = jnp.zeros((chunk, hd), F32)
        for h in range(width // hd):
            block = tbl[at, h * hd : (h + 1) * hd].astype(F32)
            squares = squares + block * block
        root = lax.rsqrt(jnp.sum(squares, axis=1, keepdims=True) * (1.0 / width) + 1e-05)
        high = root.astype(BF16).astype(F32)
        mid = (root - high).astype(BF16).astype(F32)
        low = root - high - mid
        emb[at, heads * hd : (heads + 1) * hd] = jnp.where(
            lane_chunk == 0,
            high,
            jnp.where(lane_chunk == 1, mid, jnp.where(lane_chunk == 2, low, 0.0)),
        ).astype(BF16)
        return carry

    lax.fori_loop(0, vocab // chunk, table_norm, 0)
    for hh in range(heads):
        emb[:, hh * hd : (hh + 1) * hd] = tbl[:, columns(head_of(me_p, me_s, hh))]

    pl.semaphore_wait(barrier, n_dev - 1)

    for k in range(1, plane):
        p = lax.rem(me_p + k, plane)
        remote(toks.at[me_p], toks.at[me_p], t_send, t_recv, me_z * plane + p, me_s).start()

    my_head = lax.div(me_d * rows, hd)
    to_p = lax.rem(my_head, plane)
    to_i = lax.div(my_head, plane)
    to_s = lax.div(to_i, heads)
    place = lax.rem(to_i, heads) * per_head + lax.rem(me_d, per_head)
    keep = (to_p == me_p) & (to_s == me_s)

    @pl.when(keep)
    def _():
        pltpu.make_async_copy(packed, params.at[me_s, place], w_recv.at[me_s]).start()

    @pl.when(jnp.logical_not(keep))
    def _():
        remote(
            packed,
            params.at[me_s, place],
            w_send,
            w_recv.at[me_s],
            me_z * plane + to_p,
            to_s,
        ).start()

    def give(k, carry):
        z = lax.rem(me_z + k, planes)
        remote(
            packed, params.at[me_s, place], w_send, w_recv.at[me_s], z * plane + to_p, to_s
        ).start()
        return carry

    lax.fori_loop(1, planes, give, 0)

    for k in range(1, plane):
        p = lax.rem(me_p + k, plane)
        for hh in range(heads):
            remote(
                out_grad.at[:, columns(head_of(p, me_s, hh))],
                cot.at[me_p, hh],
                c_send,
                c_recv.at[me_p],
                me_z * plane + p,
                me_s,
            ).start()

    eye = lax.broadcasted_iota(jnp.int32, (seq, seq), 0) == lax.broadcasted_iota(
        jnp.int32, (seq, seq), 1
    )

    def as_column(row):
        return jnp.sum(jnp.where(eye, row, 0.0), axis=1, keepdims=True)

    def exchange(phase, q):
        sums = jnp.sum(acc[...], axis=1, keepdims=True)
        for j in range(slots):
            own = jnp.where(eye, sums[j * seq : (j + 1) * seq], 0.0)
            parts[phase, q, member, j : j + 1, 0:seq] = jnp.sum(own, axis=0, keepdims=True)

        def share(k, carry):
            t = lax.rem(member + k, members)
            remote(
                parts.at[phase, q, member],
                parts.at[phase, q, member],
                x_send,
                x_recv.at[phase, q],
                me_z * plane + lax.div(t, n_sec),
                lax.rem(t, n_sec),
            ).start()
            return carry

        lax.fori_loop(1, members, share, 0)

    def exchanged(phase, q):
        if members > 1:
            whole = parts.at[phase, q, pl.ds(0, members - 1)]
            pltpu.make_async_copy(whole, whole, x_recv.at[phase, q]).wait()
        return jnp.sum(parts[phase, q, :, :, 0:seq], axis=0)

    def layer_param(b, hh):
        at = hh * per_head
        tail = params[b, at, rows:, :].astype(F32)
        weight = params[b, at, :rows, :]
        if per_head > 1:
            for i in range(1, per_head):
                tail = tail + params[b, at + i, rows:, :].astype(F32)
            weight = jnp.concatenate(
                [params[b, at + i, :rows, :] for i in range(per_head)], axis=0
            )
        return weight, tail[0:1], tail[1:2]

    at_row = lax.broadcasted_iota(jnp.int32, (group_rows, group_rows), 0)
    at_col = lax.broadcasted_iota(jnp.int32, (group_rows, group_rows), 1)
    allowed = at_row <= at_col
    for i in range(1, GROUP):
        allowed = allowed & ((at_row >= i * seq) == (at_col >= i * seq))
    vocab_lane = lax.broadcasted_iota(jnp.int32, (seq, vocab), 1).astype(F32)

    if plane > 1:
        pltpu.make_async_copy(
            toks.at[pl.ds(0, plane - 1)], toks.at[pl.ds(0, plane - 1)], t_recv
        ).wait()

    def embed(q, carry):
        for j in range(slots):
            col = as_column(toks[q, j : j + 1, 0:seq])
            picked[j * seq : (j + 1) * seq, :] = jnp.where(vocab_lane == col, 1.0, 0.0).astype(
                BF16
            )
        found = matmul(picked[...], emb[...], 1, 0)
        for hh in range(heads):
            xs[0, q, hh] = found[:, hh * hd : (hh + 1) * hd].astype(BF16)
        root = jnp.sum(found[:, heads * hd :], axis=1, keepdims=True)
        rstd[0, q] = jnp.broadcast_to(root, (slots * seq, hd))
        return carry

    lax.fori_loop(0, plane, embed, 0)
    for i in range(layers):
        pltpu.make_async_copy(params.at[i], params.at[i], w_recv.at[i]).wait()

    for b in range(layers):

        def forward(q, carry):
            if b > 0:
                root = lax.rsqrt(exchanged(b - 1, q) * (1.0 / width) + 1e-05)
                for j in range(slots):
                    rstd[b, q, j * seq : (j + 1) * seq, :] = jnp.broadcast_to(
                        as_column(root[j : j + 1]), (seq, hd)
                    )
            for hh in range(heads):
                weight, gain_row, scale_row = layer_param(b, hh)
                x_in = xs[b, q, hh].astype(F32)
                norm = (x_in * rstd[b, q] * gain_row).astype(BF16)
                normed[b, q, hh] = norm
                query = (matmul(norm, weight, 1, 0) * inv).astype(BF16)
                queries[b, q, hh] = query
                for i in range(groups):
                    lo, hi = i * group_rows, (i + 1) * group_rows
                    scores = matmul(norm[lo:hi], query[lo:hi], 1, 1)
                    scores = jnp.where(allowed, scores, -1e30)
                    raised = jnp.exp(scores - jnp.max(scores, axis=0, keepdims=True))
                    attend = raised * (1.0 / jnp.sum(raised, axis=0, keepdims=True))
                    probs[b, q, hh, i] = attend
                    mix = matmul(attend.astype(BF16), norm[lo:hi], 0, 0)
                    mixed[b, q, hh, lo:hi] = mix
                    if b + 1 < layers:
                        out = (x_in[lo:hi] + scale_row * mix).astype(BF16)
                        xs[b + 1, q, hh, lo:hi] = out
                        out = out.astype(F32)
                        if hh == 0:
                            acc[lo:hi] = out * out
                        else:
                            acc[lo:hi] += out * out
            if b + 1 < layers:
                exchange(b, q)
            return carry

        lax.fori_loop(0, plane, forward, 0)

    for b in reversed(range(layers)):
        for hh in range(heads):
            grads[hh] = jnp.zeros((hd, hd), F32)
            tails[hh] = jnp.zeros((8, hd), F32)

        def backward(q, carry):
            if b + 1 == layers:
                pltpu.make_async_copy(cot.at[q], cot.at[q], c_recv.at[q]).wait()
            else:
                phase = layers - 1 + b
                inner = exchanged(phase, q) * (1.0 / width)
                for j in range(slots):
                    at = slice(j * seq, (j + 1) * seq)
                    root = rstd[b + 1, q, at]
                    acc[at] = as_column(inner[j : j + 1]) * root * root * root
                for hh in range(heads):
                    _, gain_row, _ = layer_param(b + 1, hh)
                    dy = dnormed[q, hh].astype(F32) * gain_row
                    back = rstd[b + 1, q] * dy - xs[b + 1, q, hh].astype(F32) * acc[...]
                    cot[q, hh] = (cot[q, hh].astype(F32) + back).astype(BF16)
            for hh in range(heads):
                weight, gain_row, scale_row = layer_param(b, hh)
                given = cot[q, hh].astype(F32)
                scale_part = jnp.sum(given * mixed[b, q, hh], axis=0, keepdims=True)
                norm = normed[b, q, hh]
                query = queries[b, q, hh]
                dmix = (given * scale_row).astype(BF16)
                dquery_parts, dnorm_parts = [], []
                for i in range(groups):
                    lo, hi = i * group_rows, (i + 1) * group_rows
                    attend = probs[b, q, hh, i]
                    dattend = matmul(norm[lo:hi], dmix[lo:hi], 1, 1).astype(BF16).astype(F32)
                    inner = jnp.sum(dattend * attend, axis=0, keepdims=True)
                    dscore = (attend * (dattend - inner)).astype(BF16)
                    dquery_parts.append(matmul(dscore, norm[lo:hi], 0, 0).astype(BF16))
                    dnorm_parts.append(
                        matmul(dscore, query[lo:hi], 1, 0)
                        + matmul(attend.astype(BF16), dmix[lo:hi], 1, 0)
                    )
                dquery = jnp.concatenate(dquery_parts, axis=0)
                dnorm = jnp.concatenate(dnorm_parts, axis=0) + matmul(dquery, weight, 1, 1) * inv
                grads[hh] += matmul(norm, dquery, 0, 0)
                dnorm = dnorm.astype(BF16)
                if b > 0:
                    dnormed[q, hh] = dnorm
                dnorm = dnorm.astype(F32)
                x_in = xs[b, q, hh].astype(F32)
                tails[hh, 0:1] += jnp.sum(dnorm * (x_in * rstd[b, q]), axis=0, keepdims=True)
                tails[hh, 1:2] += scale_part
                if b > 0:
                    inside = dnorm * gain_row * x_in
                    if hh == 0:
                        acc[...] = inside
                    else:
                        acc[...] += inside
            if b > 0:
                exchange(layers - 2 + b, q)
            return carry

        lax.fori_loop(0, plane, backward, 0)
        for hh in range(heads):
            gain_part, scale_part = tails[hh, 0:1], tails[hh, 1:2]
            gain_hi = gain_part.astype(BF16).astype(F32)
            scale_hi = scale_part.astype(BF16).astype(F32)
            tail = jnp.where(
                tail_row == 0,
                gain_hi,
                jnp.where(
                    tail_row == 1,
                    gain_part - gain_hi,
                    jnp.where(
                        tail_row == 2,
                        scale_hi,
                        jnp.where(tail_row == 3, scale_part - scale_hi, 0.0),
                    ),
                ),
            ).astype(BF16)
            dweight = (grads[hh] * inv).astype(BF16)
            for i in range(per_head):
                at = hh * per_head + i
                tx[b, at, 0:rows] = dweight[i * rows : (i + 1) * rows]
                tx[b, at, rows : rows + TAIL] = tail
        for hh in range(heads):
            for i in range(per_head):
                at = hh * per_head + i
                r = head_of(me_p, me_s, hh) * per_head + i
                mine = (r == me_d) & (me_s == b)

                @pl.when(mine)
                def _():
                    pltpu.make_async_copy(tx.at[b, at], rx.at[me_z], g_recv).start()

                @pl.when(jnp.logical_not(mine))
                def _():
                    remote(tx.at[b, at], rx.at[me_z], g_send, g_recv, r, b).start()

    pltpu.make_async_copy(rx, rx, g_recv).wait()
    total = jnp.sum(rx[...].astype(F32), axis=0)
    total_query = total[0:rows]
    total_gain = total[rows : rows + 1] + total[rows + 1 : rows + 2]
    total_scale = total[rows + 2 : rows + 3] + total[rows + 3 : rows + 4]
    if per_head > 1:
        at = lax.broadcasted_iota(jnp.int32, (1, hd), 1)
        first = lax.rem(me_d, per_head) * rows
        inside = (at >= first) & (at < first + rows)
        total_gain = jnp.where(inside, total_gain, 0.0)
        total_scale = jnp.where(inside, total_scale, 0.0)
    squares = (
        jnp.sum(total_query * total_query, axis=0, keepdims=True)
        + total_gain * total_gain
        + total_scale * total_scale
    )
    norms[pl.ds(me, 1)] = squares[None]

    def tell(k, carry):
        t = lax.rem(me + k, n_dev)
        remote(
            norms.at[me], norms.at[me], n_send, n_recv, lax.div(t, n_sec), lax.rem(t, n_sec)
        ).start()
        return carry

    lax.fori_loop(1, n_dev, tell, 0)
    others = norms.at[pl.ds(0, n_dev - 1)]
    pltpu.make_async_copy(others, others, n_recv).wait()
    overall = jnp.sum(jnp.sum(norms[...], axis=0), axis=1, keepdims=True)
    limit = float(layers * width * (hd + 2))
    factor = jnp.minimum(1.0, math.sqrt(limit) / jnp.sqrt(overall))
    query_out[...] = total_query * factor
    gain_out[...] = total_gain * factor
    scale_out[...] = total_scale * factor

    pltpu.make_async_copy(others, others, n_send).wait()
    if members > 1:
        for phase in range(2 * layers - 2):
            whole = parts.at[phase, :, pl.ds(0, members - 1)]
            pltpu.make_async_copy(whole, whole, x_send).wait()
    if plane > 1:
        sent = toks.at[pl.ds(0, plane - 1)]
        pltpu.make_async_copy(sent, sent, t_send).wait()
        sent = cot.at[pl.ds(0, plane - 1)]
        pltpu.make_async_copy(sent, sent, c_send).wait()

    def sent_weight(k, carry):
        pltpu.make_async_copy(packed, packed, w_send).wait()
        return carry

    lax.fori_loop(0, jnp.where(keep, planes - 1, planes), sent_weight, 0)

    def sent_grad(k, carry):
        pltpu.make_async_copy(packed, packed, g_send).wait()
        return carry

    pieces = layers * heads * per_head
    lax.fori_loop(0, jnp.where(keep, pieces - 1, pieces), sent_grad, 0)


def on_device(path_table, tokens, assign, out_grad, query_weights, gain, scale):
    n_dp = lax.axis_size("dp")
    n_sec = lax.axis_size("section")
    vocab, width = path_table.shape
    slots, seq = tokens.shape[1:]
    rows, hd = query_weights.shape[1:]
    count = slots * seq
    layers = n_sec
    plane, planes, heads = layout(n_dp, n_sec, width, hd)
    per_head = hd // rows
    pieces = heads * per_head
    n_dev = n_dp * n_sec
    groups = slots // GROUP
    first = lax.rem(lax.axis_index("dp") * rows, hd)
    if rows < hd:
        gain = lax.dynamic_update_slice(jnp.zeros((1, hd), BF16), gain, (0, first))
        scale = lax.dynamic_update_slice(jnp.zeros((1, hd), BF16), scale, (0, first))
    vmem = pl.BlockSpec(memory_space=pltpu.VMEM)
    hbm = pl.BlockSpec(memory_space=pl.ANY)
    smem = pl.BlockSpec(memory_space=pltpu.SMEM)
    query_grad, gain_grad, scale_grad = pl.pallas_call(
        functools.partial(step_kernel, n_dp, n_sec),
        out_shape=(
            jax.ShapeDtypeStruct((rows, hd), F32),
            jax.ShapeDtypeStruct((1, hd), F32),
            jax.ShapeDtypeStruct((1, hd), F32),
        ),
        in_specs=[hbm, vmem, smem, hbm, vmem, vmem, vmem],
        out_specs=(vmem, vmem, vmem),
        scratch_shapes=[
            pltpu.VMEM((rows + TAIL, hd), BF16),
            pltpu.VMEM((layers, pieces, rows + TAIL, hd), BF16),
            pltpu.VMEM((plane, slots, hd), F32),
            pltpu.VMEM((count, vocab), BF16),
            pltpu.VMEM((vocab, width), BF16),
            pltpu.VMEM((vocab, (heads + 1) * hd), BF16),
            pltpu.VMEM((plane, heads, count, hd), BF16),
            pltpu.VMEM((layers, plane, heads, count, hd), BF16),
            pltpu.VMEM((layers, plane, heads, count, hd), BF16),
            pltpu.VMEM((layers, plane, heads, count, hd), BF16),
            pltpu.VMEM((layers, plane, heads, count, hd), F32),
            pltpu.VMEM((layers, plane, heads, groups, GROUP * seq, GROUP * seq), F32),
            pltpu.VMEM((plane, heads, count, hd), BF16),
            pltpu.VMEM((count, hd), F32),
            pltpu.VMEM((layers, plane, count, hd), F32),
            pltpu.VMEM((max(1, 2 * layers - 2), plane, plane * n_sec, slots, hd), F32),
            pltpu.VMEM((heads, hd, hd), F32),
            pltpu.VMEM((heads, 8, hd), F32),
            pltpu.VMEM((layers, pieces, rows + TAIL, hd), BF16),
            pltpu.VMEM((planes, rows + TAIL, hd), BF16),
            pltpu.VMEM((n_dev, 1, hd), F32),
            pltpu.SemaphoreType.DMA,
            pltpu.SemaphoreType.DMA,
            pltpu.SemaphoreType.DMA,
            pltpu.SemaphoreType.DMA,
            pltpu.SemaphoreType.DMA((layers,)),
            pltpu.SemaphoreType.DMA,
            pltpu.SemaphoreType.DMA((plane,)),
            pltpu.SemaphoreType.DMA,
            pltpu.SemaphoreType.DMA((max(1, 2 * layers - 2), plane)),
            pltpu.SemaphoreType.DMA,
            pltpu.SemaphoreType.DMA,
            pltpu.SemaphoreType.DMA,
            pltpu.SemaphoreType.DMA,
        ],
        compiler_params=pltpu.CompilerParams(
            collective_id=0, has_side_effects=True, vmem_limit_bytes=56 * 1024 * 1024
        ),
    )(
        path_table,
        tokens[0],
        assign[0],
        out_grad.reshape(count, width),
        query_weights[0],
        gain,
        scale,
    )
    if rows < hd:
        gain_grad = lax.dynamic_slice(gain_grad, (0, first), (1, rows))
        scale_grad = lax.dynamic_slice(scale_grad, (0, first), (1, rows))
    return query_grad[None], gain_grad, scale_grad


def solution(mesh):
    in_specs = (
        P(),
        P("dp", None, None),
        P("dp", None),
        P("dp", None, None, None, None),
        P("section", "dp", None),
        P("section", "dp"),
        P("section", "dp"),
    )
    out_specs = (P("section", "dp", None), P("section", "dp"), P("section", "dp"))
    return jax.shard_map(
        on_device, mesh=mesh, in_specs=in_specs, out_specs=out_specs, check_vma=False
    )
```

time: 74.2 us -> 61.9 us (0.83)
  Pallas kernels: 69.6 us -> 57.2 us
    pallas_call x1, Pallas kernels: 69.6 us -> 57.2 us  [on_device(): pl.pallas_call(functools.partial(step_kernel, n_dp, n_sec), out_shape=(ja...]
where the time goes in v2:
time: 61.9 us; the launch traced here: 61.6 us
  Pallas kernels  57.2 us (92%)
  local copies, waits for them, and re-layouts  3.7 us (6%)
  between operations  0.64 us (1%)
    pallas_call x1, Pallas kernels, on_device(): pl.pallas_call(functools.partial(step_kernel, n_dp, n_sec), out_shape=(ja...  57.2 us
    unnamed x3, local copies, waits for them, and re-layouts  3.7 us

profile of v2, /device:TPU:0, one launch (start us, length us, event | category | flops | bytes accessed | tf_op | source)
XLA Modules:
  0.0 61.6 jit_solution(16305953968626056256)
XLA Ops:
  0.6 57.2 %shard_map.94 = (f32[128,128]{1,0:T(8,128)}, f32[1,128]{1,0:T(1,128)}, f32[1,128]{1,0:T(1,128)}) custom-call(bf16[512,2048]{1,0:T(8,128)(2,1)} %table.1, s32[8,48]{1,0:T(8,128)} %bitcast.8, s32[8]{0:T(128)} %bitcast.9, bf16[384,2048]{1,0:T(8,128)(2,1)} %bitcast.5, bf16[128,128]{1,0:T(8,128)(2,1)} %bitcast.7, bf16[1,128]{1,0:T(2,128)(2,1)} %gain.1, ...), custom_call_target="tpu_custom_call" | custom-call | tf_op jit(solution)/shard_map/pallas_call | solution.py:505
  57.9 1.5 %copy.13 = f32[1,128,128]{2,1,0:T(8,128)} copy(f32[1,128,128]{2,1,0:T(8,128)} %bitcast.6) | data formatting | bytes 131072
  59.4 1.1 %copy.14 = f32[1,128]{1,0:T(1,128)} copy(f32[1,128]{1,0:T(1,128)} %get-tuple-element.13) | data formatting | bytes 1024
  60.5 1.1 %copy.15 = f32[1,128]{1,0:T(1,128)} copy(f32[1,128]{1,0:T(1,128)} %get-tuple-element.14) | data formatting | bytes 1024

commit v3 on v2

--- a/solution.py
+++ b/solution.py
@@ -14,6 +14,7 @@
 TAIL = 16
 GROUP = 2
 PLANE = 4
+AHEAD = 4
 
 
 def matmul(lhs, rhs, lhs_dim, rhs_dim):
@@ -37,9 +38,7 @@
     weights,
     gain,
     scale,
-    query_out,
-    gain_out,
-    scale_out,
+    out,
     packed,
     params,
     toks,
@@ -284,10 +283,9 @@
         return carry
 
     lax.fori_loop(0, plane, embed, 0)
-    for i in range(layers):
-        pltpu.make_async_copy(params.at[i], params.at[i], w_recv.at[i]).wait()
 
     for b in range(layers):
+        pltpu.make_async_copy(params.at[b], params.at[b], w_recv.at[b]).wait()
 
         def forward(q, carry):
             if b > 0:
@@ -296,30 +294,45 @@
                     rstd[b, q, j * seq : (j + 1) * seq, :] = jnp.broadcast_to(
                         as_column(root[j : j + 1]), (seq, hd)
                     )
+            held = []
             for hh in range(heads):
                 weight, gain_row, scale_row = layer_param(b, hh)
-                x_in = xs[b, q, hh].astype(F32)
-                norm = (x_in * rstd[b, q] * gain_row).astype(BF16)
+                norm = (xs[b, q, hh].astype(F32) * rstd[b, q] * gain_row).astype(BF16)
                 normed[b, q, hh] = norm
                 query = (matmul(norm, weight, 1, 0) * inv).astype(BF16)
                 queries[b, q, hh] = query
-                for i in range(groups):
-                    lo, hi = i * group_rows, (i + 1) * group_rows
-                    scores = matmul(norm[lo:hi], query[lo:hi], 1, 1)
-                    scores = jnp.where(allowed, scores, -1e30)
-                    raised = jnp.exp(scores - jnp.max(scores, axis=0, keepdims=True))
-                    attend = raised * (1.0 / jnp.sum(raised, axis=0, keepdims=True))
+                held.append((norm, query, scale_row))
+            tiles = [
+                (hh, i, i * group_rows, (i + 1) * group_rows)
+                for hh in range(heads)
+                for i in range(groups)
+            ]
+            for some in [tiles[at : at + AHEAD] for at in range(0, len(tiles), AHEAD)]:
+                scores = [
+                    matmul(held[hh][0][lo:hi], held[hh][1][lo:hi], 1, 1) for hh, i, lo, hi in some
+                ]
+                scores = [jnp.where(allowed, one, -1e30) for one in scores]
+                tops = [jnp.max(one, axis=0, keepdims=True) for one in scores]
+                raised = [jnp.exp(one - top) for one, top in zip(scores, tops)]
+                sums = [1.0 / jnp.sum(one, axis=0, keepdims=True) for one in raised]
+                attends = [one * part for one, part in zip(raised, sums)]
+                for (hh, i, lo, hi), attend in zip(some, attends):
                     probs[b, q, hh, i] = attend
-                    mix = matmul(attend.astype(BF16), norm[lo:hi], 0, 0)
+                mixes = [
+                    matmul(attend.astype(BF16), held[hh][0][lo:hi], 0, 0)
+                    for (hh, i, lo, hi), attend in zip(some, attends)
+                ]
+                for (hh, i, lo, hi), mix in zip(some, mixes):
                     mixed[b, q, hh, lo:hi] = mix
                     if b + 1 < layers:
-                        out = (x_in[lo:hi] + scale_row * mix).astype(BF16)
-                        xs[b + 1, q, hh, lo:hi] = out
-                        out = out.astype(F32)
+                        out_rows = xs[b, q, hh, lo:hi].astype(F32) + held[hh][2] * mix
+                        out_rows = out_rows.astype(BF16)
+                        xs[b + 1, q, hh, lo:hi] = out_rows
+                        out_rows = out_rows.astype(F32)
                         if hh == 0:
-                            acc[lo:hi] = out * out
+                            acc[lo:hi] = out_rows * out_rows
                         else:
-                            acc[lo:hi] += out * out
+                            acc[lo:hi] += out_rows * out_rows
             if b + 1 < layers:
                 exchange(b, q)
             return carry
@@ -353,18 +366,31 @@
                 norm = normed[b, q, hh]
                 query = queries[b, q, hh]
                 dmix = (given * scale_row).astype(BF16)
+                cuts = [(i, i * group_rows, (i + 1) * group_rows) for i in range(groups)]
                 dquery_parts, dnorm_parts = [], []
-                for i in range(groups):
-                    lo, hi = i * group_rows, (i + 1) * group_rows
-                    attend = probs[b, q, hh, i]
-                    dattend = matmul(norm[lo:hi], dmix[lo:hi], 1, 1).astype(BF16).astype(F32)
-                    inner = jnp.sum(dattend * attend, axis=0, keepdims=True)
-                    dscore = (attend * (dattend - inner)).astype(BF16)
-                    dquery_parts.append(matmul(dscore, norm[lo:hi], 0, 0).astype(BF16))
-                    dnorm_parts.append(
+                for some in [cuts[at : at + AHEAD] for at in range(0, len(cuts), AHEAD)]:
+                    datts = [
+                        matmul(norm[lo:hi], dmix[lo:hi], 1, 1).astype(BF16).astype(F32)
+                        for i, lo, hi in some
+                    ]
+                    attends = [probs[b, q, hh, i] for i, lo, hi in some]
+                    inners = [
+                        jnp.sum(datt * attend, axis=0, keepdims=True)
+                        for datt, attend in zip(datts, attends)
+                    ]
+                    dscores = [
+                        (attend * (datt - inner)).astype(BF16)
+                        for datt, attend, inner in zip(datts, attends, inners)
+                    ]
+                    dquery_parts += [
+                        matmul(dscore, norm[lo:hi], 0, 0).astype(BF16)
+                        for (i, lo, hi), dscore in zip(some, dscores)
+                    ]
+                    dnorm_parts += [
                         matmul(dscore, query[lo:hi], 1, 0)
                         + matmul(attend.astype(BF16), dmix[lo:hi], 1, 0)
-                    )
+                        for (i, lo, hi), dscore, attend in zip(some, dscores, attends)
+                    ]
                 dquery = jnp.concatenate(dquery_parts, axis=0)
                 dnorm = jnp.concatenate(dnorm_parts, axis=0) + matmul(dquery, weight, 1, 1) * inv
                 grads[hh] += matmul(norm, dquery, 0, 0)
@@ -453,9 +479,10 @@
     overall = jnp.sum(jnp.sum(norms[...], axis=0), axis=1, keepdims=True)
     limit = float(layers * width * (hd + 2))
     factor = jnp.minimum(1.0, math.sqrt(limit) / jnp.sqrt(overall))
-    query_out[...] = total_query * factor
-    gain_out[...] = total_gain * factor
-    scale_out[...] = total_scale * factor
+    out[0:rows] = total_query * factor
+    out[rows : rows + 8] = jnp.where(
+        lax.broadcasted_iota(jnp.int32, (8, hd), 0) == 0, total_gain * factor, total_scale * factor
+    )
 
     pltpu.make_async_copy(others, others, n_send).wait()
     if members > 1:
@@ -502,15 +529,11 @@
     vmem = pl.BlockSpec(memory_space=pltpu.VMEM)
     hbm = pl.BlockSpec(memory_space=pl.ANY)
     smem = pl.BlockSpec(memory_space=pltpu.SMEM)
-    query_grad, gain_grad, scale_grad = pl.pallas_call(
+    found = pl.pallas_call(
         functools.partial(step_kernel, n_dp, n_sec),
-        out_shape=(
-            jax.ShapeDtypeStruct((rows, hd), F32),
-            jax.ShapeDtypeStruct((1, hd), F32),
-            jax.ShapeDtypeStruct((1, hd), F32),
-        ),
+        out_shape=jax.ShapeDtypeStruct((rows + 8, hd), F32),
         in_specs=[hbm, vmem, smem, hbm, vmem, vmem, vmem],
-        out_specs=(vmem, vmem, vmem),
+        out_specs=vmem,
         scratch_shapes=[
             pltpu.VMEM((rows + TAIL, hd), BF16),
             pltpu.VMEM((layers, pieces, rows + TAIL, hd), BF16),
@@ -559,6 +582,8 @@
         gain,
         scale,
     )
+    query_grad = found[:rows]
+    gain_grad, scale_grad = found[rows : rows + 1], found[rows + 1 : rows + 2]
     if rows < hd:
         gain_grad = lax.dynamic_slice(gain_grad, (0, first), (1, rows))
         scale_grad = lax.dynamic_slice(scale_grad, (0, first), (1, rows))

time: 61.9 us -> 46.1 us (0.74)
  Pallas kernels: 57.2 us -> 42.4 us
  local copies, waits for them, and re-layouts: 3.7 us -> 2.75 us
    pallas_call x1, Pallas kernels: 57.2 us -> 42.4 us  [on_device(): pl.pallas_call(functools.partial(step_kernel, n_dp, n_sec), out_shape=jax...]
    unnamed x3 -> x0, local copies, waits for them, and re-layouts: 3.7 us -> none
    broadcast_in_dim x0 -> x1, local copies, waits for them, and re-layouts: none -> 1.47 us  [on_device(): return (query_grad[None], gain_grad, scale_grad)]
    slice x0 -> x1, local copies, waits for them, and re-layouts: none -> 1.27 us  [on_device(): gain_grad, scale_grad = (found[rows:rows + 1], found[rows + 1:rows + 2])]
where the time goes in v3:
time: 46.1 us; the launch traced here: 45.8 us
  Pallas kernels  42.4 us (92%)
  local copies, waits for them, and re-layouts  2.75 us (6%)
  between operations  0.64 us (1%)
    pallas_call x1, Pallas kernels, on_device(): pl.pallas_call(functools.partial(step_kernel, n_dp, n_sec), out_shape=jax...  42.4 us
    broadcast_in_dim x1, local copies, waits for them, and re-layouts, on_device(): return (query_grad[None], gain_grad, scale_grad)  1.47 us
    slice x1, local copies, waits for them, and re-layouts, on_device(): gain_grad, scale_grad = (found[rows:rows + 1], found[rows + 1:rows + 2])  1.27 us

profile of v3, /device:TPU:0, one launch (start us, length us, event | category | flops | bytes accessed | tf_op | source)
XLA Modules:
  0.0 45.8 jit_solution(17276153608716247920)
XLA Ops:
  0.6 42.4 %shard_map.94 = f32[136,128]{1,0:T(8,128)} custom-call(bf16[512,2048]{1,0:T(8,128)(2,1)} %table.1, s32[8,48]{1,0:T(8,128)} %bitcast.8, s32[8]{0:T(128)} %bitcast.9, bf16[384,2048]{1,0:T(8,128)(2,1)} %bitcast.6, bf16[128,128]{1,0:T(8,128)(2,1)} %bitcast.7, bf16[1,128]{1,0:T(2,128)(2,1)} %gain.1, bf16[1,128]{1,0:T(2,128)(2,1)} %scale.1), custom_call_target="tpu_custom_call" | custom-call | tf_op jit(solution)/shard_map/pallas_call | solution.py:532
  43.0 1.3 %fusion = (f32[1,128]{1,0:T(1,128)}, f32[1,128]{1,0:T(1,128)}) fusion(f32[136,128]{1,0:T(8,128)} %shard_map.94), kind=kLoop, calls=%fused_computation.1 | loop fusion | bytes 2048 | tf_op jit(solution)/shard_map/slice | solution.py:586
  44.3 1.5 %slice_bitcast_fusion = f32[1,128,128]{2,1,0:T(8,128)} fusion(f32[136,128]{1,0:T(8,128)} %shard_map.94), kind=kLoop, calls=%fused_computation | loop fusion | bytes 131072 | tf_op jit(solution)/shard_map/broadcast_in_dim | solution.py:590

commit v4 on v3

--- a/solution.py
+++ b/solution.py
@@ -14,7 +14,7 @@
 TAIL = 16
 GROUP = 2
 PLANE = 4
-AHEAD = 4
+AHEAD = 8
 
 
 def matmul(lhs, rhs, lhs_dim, rhs_dim):
@@ -359,48 +359,55 @@
                     dy = dnormed[q, hh].astype(F32) * gain_row
                     back = rstd[b + 1, q] * dy - xs[b + 1, q, hh].astype(F32) * acc[...]
                     cot[q, hh] = (cot[q, hh].astype(F32) + back).astype(BF16)
+            held = []
             for hh in range(heads):
                 weight, gain_row, scale_row = layer_param(b, hh)
                 given = cot[q, hh].astype(F32)
-                scale_part = jnp.sum(given * mixed[b, q, hh], axis=0, keepdims=True)
-                norm = normed[b, q, hh]
-                query = queries[b, q, hh]
-                dmix = (given * scale_row).astype(BF16)
+                tails[hh, 1:2] += jnp.sum(given * mixed[b, q, hh], axis=0, keepdims=True)
+                held.append((weight, gain_row, (given * scale_row).astype(BF16)))
+            dqueries, dnorms = [], []
+            for hh in range(heads):
+                dmix = held[hh][2]
                 cuts = [(i, i * group_rows, (i + 1) * group_rows) for i in range(groups)]
-                dquery_parts, dnorm_parts = [], []
-                for some in [cuts[at : at + AHEAD] for at in range(0, len(cuts), AHEAD)]:
-                    datts = [
-                        matmul(norm[lo:hi], dmix[lo:hi], 1, 1).astype(BF16).astype(F32)
-                        for i, lo, hi in some
+                datts = [
+                    matmul(normed[b, q, hh, lo:hi], dmix[lo:hi], 1, 1)
+                    .astype(BF16)
+                    .astype(F32)
+                    for i, lo, hi in cuts
+                ]
+                attends = [probs[b, q, hh, i] for i, lo, hi in cuts]
+                inners = [
+                    jnp.sum(datt * attend, axis=0, keepdims=True)
+                    for datt, attend in zip(datts, attends)
+                ]
+                dscores = [
+                    (attend * (datt - inner)).astype(BF16)
+                    for datt, attend, inner in zip(datts, attends, inners)
+                ]
+                dqueries.append(
+                    [
+                        matmul(dscore, normed[b, q, hh, lo:hi], 0, 0).astype(BF16)
+                        for (i, lo, hi), dscore in zip(cuts, dscores)
                     ]
-                    attends = [probs[b, q, hh, i] for i, lo, hi in some]
-                    inners = [
-                        jnp.sum(datt * attend, axis=0, keepdims=True)
-                        for datt, attend in zip(datts, attends)
+                )
+                dnorms.append(
+                    [
+                        matmul(dscore, queries[b, q, hh, lo:hi], 1, 0)
+                        + matmul(attend.astype(BF16), dmix[lo:hi], 1, 0)
+                        for (i, lo, hi), dscore, attend in zip(cuts, dscores, attends)
                     ]
-                    dscores = [
-                        (attend * (datt - inner)).astype(BF16)
-                        for datt, attend, inner in zip(datts, attends, inners)
-                    ]
-                    dquery_parts += [
-                        matmul(dscore, norm[lo:hi], 0, 0).astype(BF16)
-                        for (i, lo, hi), dscore in zip(some, dscores)
-                    ]
-                    dnorm_parts += [
-                        matmul(dscore, query[lo:hi], 1, 0)
-                        + matmul(attend.astype(BF16), dmix[lo:hi], 1, 0)
-                        for (i, lo, hi), dscore, attend in zip(some, dscores, attends)
-                    ]
-                dquery = jnp.concatenate(dquery_parts, axis=0)
-                dnorm = jnp.concatenate(dnorm_parts, axis=0) + matmul(dquery, weight, 1, 1) * inv
-                grads[hh] += matmul(norm, dquery, 0, 0)
+                )
+            for hh in range(heads):
+                weight, gain_row, _ = held[hh]
+                dquery = jnp.concatenate(dqueries[hh], axis=0)
+                dnorm = jnp.concatenate(dnorms[hh], axis=0) + matmul(dquery, weight, 1, 1) * inv
+                grads[hh] += matmul(normed[b, q, hh], dquery, 0, 0)
                 dnorm = dnorm.astype(BF16)
                 if b > 0:
                     dnormed[q, hh] = dnorm
                 dnorm = dnorm.astype(F32)
                 x_in = xs[b, q, hh].astype(F32)
                 tails[hh, 0:1] += jnp.sum(dnorm * (x_in * rstd[b, q]), axis=0, keepdims=True)
-                tails[hh, 1:2] += scale_part
                 if b > 0:
                     inside = dnorm * gain_row * x_in
                     if hh == 0:

time: 46.1 us -> 44.7 us (0.970)
  Pallas kernels: 42.4 us -> 41 us
    pallas_call x1, Pallas kernels: 42.4 us -> 41 us  [on_device(): pl.pallas_call(functools.partial(step_kernel, n_dp, n_sec), out_shape=jax...]
where the time goes in v4:
time: 44.7 us; the launch traced here: 44.4 us
  Pallas kernels  41 us (92%)
  local copies, waits for them, and re-layouts  2.75 us (6%)
  between operations  0.64 us (1%)
    pallas_call x1, Pallas kernels, on_device(): pl.pallas_call(functools.partial(step_kernel, n_dp, n_sec), out_shape=jax...  41 us
    broadcast_in_dim x1, local copies, waits for them, and re-layouts, on_device(): return (query_grad[None], gain_grad, scale_grad)  1.47 us
    slice x1, local copies, waits for them, and re-layouts, on_device(): gain_grad, scale_grad = (found[rows:rows + 1], found[rows + 1:rows + 2])  1.27 us

profile of v4, /device:TPU:0, one launch (start us, length us, event | category | flops | bytes accessed | tf_op | source)
XLA Modules:
  0.0 44.4 jit_solution(3973866668881423944)
XLA Ops:
  0.6 41.0 %shard_map.94 = f32[136,128]{1,0:T(8,128)} custom-call(bf16[512,2048]{1,0:T(8,128)(2,1)} %table.1, s32[8,48]{1,0:T(8,128)} %bitcast.8, s32[8]{0:T(128)} %bitcast.9, bf16[384,2048]{1,0:T(8,128)(2,1)} %bitcast.6, bf16[128,128]{1,0:T(8,128)(2,1)} %bitcast.7, bf16[1,128]{1,0:T(2,128)(2,1)} %gain.1, bf16[1,128]{1,0:T(2,128)(2,1)} %scale.1), custom_call_target="tpu_custom_call" | custom-call | tf_op jit(solution)/shard_map/pallas_call | solution.py:539
  41.7 1.3 %fusion = (f32[1,128]{1,0:T(1,128)}, f32[1,128]{1,0:T(1,128)}) fusion(f32[136,128]{1,0:T(8,128)} %shard_map.94), kind=kLoop, calls=%fused_computation.1 | loop fusion | bytes 2048 | tf_op jit(solution)/shard_map/slice | solution.py:593
  43.0 1.5 %slice_bitcast_fusion = f32[1,128,128]{2,1,0:T(8,128)} fusion(f32[136,128]{1,0:T(8,128)} %shard_map.94), kind=kLoop, calls=%fused_computation | loop fusion | bytes 131072 | tf_op jit(solution)/shard_map/broadcast_in_dim | solution.py:597
